TPU v7x, 32 devices: a whole 2x2x4 slice. The times are simulated.
32 devices in a mesh: dp: 16 (over z, y, x), tile: 2 (over core).
Axes of the slice: x: 2, y: 2, z: 4, core: 2. Of those that a mesh axis runs over, the one named last changes fastest.
Arguments:
- layer_input: bfloat16 [49152, 768], P(('dp', 'tile')), may hold values from -32 to 32
- segment_ids: int32 [49152], P(('dp', 'tile')), may hold values from 0 to 11, as said below
- pad_mask: int32 [49152], P(('dp', 'tile')), may hold values from 0 to 1, as said below
- pair_slots: int32 [192, 2], P('dp'), may hold values from 0 to 23, as said below
- result_cotangent: bfloat16 [49152, 768], P(('dp', 'tile')), may hold values from -0.059814453 to 0.059814453
- query_weight: bfloat16 [768, 768], P(('dp', 'tile')), may hold values from -0.21875 to 0.21875
- key_weight: bfloat16 [768, 768], P(('dp', 'tile')), may hold values from -0.21875 to 0.21875
- value_weight: bfloat16 [768, 768], P(('dp', 'tile')), may hold values from -0.21875 to 0.21875
- output_weight: bfloat16 [768, 768], P(('dp', 'tile')), may hold values from -0.875 to 0.875
- query_bias: bfloat16 [768], P(('dp', 'tile')), may hold values from -3 to 3
- value_bias: bfloat16 [768], P(('dp', 'tile')), may hold values from -0.59765625 to 0.59765625
- output_bias: bfloat16 [768], P(('dp', 'tile')), may hold values from -1.796875 to 1.796875
- first_gain: bfloat16 [768], P(('dp', 'tile')), may hold values from 0.5 to 1.5
- first_shift: bfloat16 [768], P(('dp', 'tile')), may hold values from -0.59765625 to 0.59765625
- inner_weight: bfloat16 [768, 3072], P(('dp', 'tile')), may hold values from -0.21875 to 0.21875
- inner_bias: bfloat16 [3072], P(('dp', 'tile')), may hold values from -1.796875 to 1.796875
- outer_weight: bfloat16 [3072, 768], P(('dp', 'tile')), may hold values from -0.109375 to 0.109375
- outer_bias: bfloat16 [768], P(('dp', 'tile')), may hold values from -1.1953125 to 1.1953125
- second_gain: bfloat16 [768], P(('dp', 'tile')), may hold values from 0.5 to 1.5
- second_shift: bfloat16 [768], P(('dp', 'tile')), may hold values from -0.59765625 to 0.59765625
Outputs:
- total_loss: float32 [], replicated
- dim_losses: float32 [5], replicated
- layer_out: bfloat16 [49152, 768], P(('dp', 'tile'))
- input_grad: float32 [49152, 768], P(('dp', 'tile'))
- query_weight_grad: float32 [768, 768], P(('dp', 'tile'))
- key_weight_grad: float32 [768, 768], P(('dp', 'tile'))
- value_weight_grad: float32 [768, 768], P(('dp', 'tile'))
- output_weight_grad: float32 [768, 768], P(('dp', 'tile'))
- query_bias_grad: float32 [768], P(('dp', 'tile'))
- value_bias_grad: float32 [768], P(('dp', 'tile'))
- output_bias_grad: float32 [768], P(('dp', 'tile'))
- first_gain_grad: float32 [768], P(('dp', 'tile'))
- first_shift_grad: float32 [768], P(('dp', 'tile'))
- inner_weight_grad: float32 [768, 3072], P(('dp', 'tile'))
- inner_bias_grad: float32 [3072], P(('dp', 'tile'))
- outer_weight_grad: float32 [3072, 768], P(('dp', 'tile'))
- outer_bias_grad: float32 [768], P(('dp', 'tile'))
- second_gain_grad: float32 [768], P(('dp', 'tile'))
- second_shift_grad: float32 [768], P(('dp', 'tile'))
Inputs may be any that keep to these rules, and one draw needn't show every extreme that they name: `segment_ids`: in each device's block of 1536 rows the ids never fall; every id 0 to 11 names a sentence of 8 to 512 rows with pad_mask 1; rows with pad_mask 0 come after the last sentence and carry id 12 - 1; some sentence has exactly 512 rows. `pad_mask`: 1 on a leading run of each device's block of 1536 rows, 0 after it. `pair_slots`: each aligned block of 12 rows holds every number 0 to 23 exactly once.
All inputs are finite; a program needn't handle non-finite values.
Results may differ from a plain program's by a relative error of at most 0.017.
Values may be sent and summed in bfloat16 or wider, within the bound.
No kernel may reach another device: no remote copies, remote signals or barrier semaphores. Data moves between devices by JAX's collectives and lax.ppermute only.
A program may use at most 192 MiB of HBM per device.

v0:
```python
from functools import partial

import jax
import jax.numpy as jnp
from jax import lax
from jax.sharding import PartitionSpec as P

D = 768
HEADS = 12
HEAD_DIM = 64
QBLOCK = 512


EPS_NORM = 1e-12
EPS_UNIT = 1e-06
INV_TEMP = 20.0
NEG_FILL = -1e30
HIGH = lax.Precision.HIGHEST


def exact_gelu(value):
    return jax.nn.gelu(value, approximate=False)


def layer_norm(value, gain, shift):
    center = value - jnp.mean(value, axis=-1, keepdims=True)
    spread = jnp.mean(center * center, axis=-1, keepdims=True)
    return center * lax.rsqrt(spread + EPS_NORM) * gain + shift


def unit_rows(value, width):
    front = value[:, :width]
    return front * lax.rsqrt(jnp.sum(front * front, axis=1, keepdims=True) + EPS_UNIT)


def column_sum(left, right):
    return lax.dot_general(
        left, right, (((0,), (0,)), ((), ())), preferred_element_type=jnp.float32
    )


def column_sum_exact(left, right):
    return lax.dot_general(
        left, right, (((0,), (0,)), ((), ())), precision=HIGH, preferred_element_type=jnp.float32
    )


def against(grad, weight):
    return lax.dot_general(
        grad, weight, (((1,), (1,)), ((), ())), preferred_element_type=jnp.float32
    )


def to_pairs(value, pair_heads):
    return value.reshape(value.shape[0], pair_heads, value.shape[1] // pair_heads).transpose(
        1, 0, 2
    )


def from_pairs(value):
    return value.transpose(1, 0, 2).reshape(value.shape[1], -1)


def masked_scores(heads, key_heads, block_segments, segment_ids, valid):
    scores = jnp.einsum(
        "qhd,khd->hqk", heads, key_heads, preferred_element_type=jnp.float32
    ) * HEAD_DIM ** (-0.5)
    allowed = (block_segments[:, None] == segment_ids[None, :]) & valid[None, :]
    return jnp.where(allowed[None], scores, NEG_FILL)


def attend_forward(query_pairs, key_pairs, value_pairs, segment_ids, valid):
    rows = query_pairs.shape[1]
    blocks = rows // QBLOCK
    query_segments = segment_ids.reshape(blocks, QBLOCK)

    def per_pair(operands):
        query_pair, key_pair, value_pair = operands
        key_heads = key_pair.reshape(rows, 2, HEAD_DIM)
        value_heads = value_pair.reshape(rows, 2, HEAD_DIM)

        def per_block(item):
            query_block, block_segments = item
            heads = query_block.reshape(QBLOCK, 2, HEAD_DIM)
            scores = masked_scores(heads, key_heads, block_segments, segment_ids, valid)
            peak = jnp.max(scores, axis=2, keepdims=True)
            expos = jnp.exp(scores - peak)
            totals = jnp.sum(expos, axis=2, keepdims=True)
            probs = (expos / totals).astype(jnp.bfloat16)
            mixed = jnp.einsum(
                "hqk,khd->qhd", probs, value_heads, preferred_element_type=jnp.float32
            )
            return (
                mixed.astype(jnp.bfloat16).reshape(QBLOCK, 2 * HEAD_DIM),
                peak + jnp.log(totals),
            )

        return lax.map(
            per_block, (query_pair.reshape(blocks, QBLOCK, 2 * HEAD_DIM), query_segments)
        )

    mixed, log_totals = lax.map(per_pair, (query_pairs, key_pairs, value_pairs))
    return (mixed.reshape(mixed.shape[0], rows, 2 * HEAD_DIM), log_totals)


def attend_backward(
    query_pairs, key_pairs, value_pairs, grad_pairs, log_totals, segment_ids, valid
):
    rows = query_pairs.shape[1]
    blocks = rows // QBLOCK
    scale = HEAD_DIM ** (-0.5)
    query_segments = segment_ids.reshape(blocks, QBLOCK)

    def per_pair(operands):
        query_pair, key_pair, value_pair, grad_pair, pair_totals = operands
        key_heads = key_pair.reshape(rows, 2, HEAD_DIM)
        value_heads = value_pair.reshape(rows, 2, HEAD_DIM)

        def per_block(carry, item):
            key_grad, value_grad = carry
            query_block, grad_block, block_totals, block_segments = item
            heads = query_block.reshape(QBLOCK, 2, HEAD_DIM)
            grads = grad_block.reshape(QBLOCK, 2, HEAD_DIM)
            scores = masked_scores(heads, key_heads, block_segments, segment_ids, valid)
            probs = jnp.exp(scores - block_totals)
            value_grad = value_grad + jnp.einsum(
                "hqk,qhd->khd",
                probs.astype(jnp.bfloat16),
                grads,
                preferred_element_type=jnp.float32,
            )
            prob_grad = jnp.einsum(
                "qhd,khd->hqk", grads, value_heads, preferred_element_type=jnp.float32
            )
            score_grad = (
                probs * (prob_grad - jnp.sum(probs * prob_grad, axis=2, keepdims=True))
            ).astype(jnp.bfloat16)
            query_grad = (
                jnp.einsum(
                    "hqk,khd->qhd", score_grad, key_heads, preferred_element_type=jnp.float32
                )
                * scale
            )
            key_grad = (
                key_grad
                + jnp.einsum("hqk,qhd->khd", score_grad, heads, preferred_element_type=jnp.float32)
                * scale
            )
            return (
                (key_grad, value_grad),
                query_grad.astype(jnp.bfloat16).reshape(QBLOCK, 2 * HEAD_DIM),
            )

        zeros = jnp.zeros((rows, 2, HEAD_DIM), jnp.float32)
        (key_grad, value_grad), query_grad = lax.scan(
            per_block,
            (zeros, zeros),
            (
                query_pair.reshape(blocks, QBLOCK, 2 * HEAD_DIM),
                grad_pair.reshape(blocks, QBLOCK, 2 * HEAD_DIM),
                pair_totals,
                query_segments,
            ),
        )
        return (
            query_grad.reshape(rows, 2 * HEAD_DIM),
            key_grad.astype(jnp.bfloat16).reshape(rows, 2 * HEAD_DIM),
            value_grad.astype(jnp.bfloat16).reshape(rows, 2 * HEAD_DIM),
        )

    return lax.map(per_pair, (query_pairs, key_pairs, value_pairs, grad_pairs, log_totals))


def attention_weights(
    query_weight,
    key_weight,
    value_weight,
    output_weight,
    query_bias,
    value_bias,
    output_bias,
    first_gain,
    first_shift,
):
    return (
        lax.all_gather(query_weight, ("dp", "tile"), axis=0, tiled=True),
        lax.all_gather(key_weight, ("dp", "tile"), axis=0, tiled=True),
        lax.all_gather(value_weight, ("dp", "tile"), axis=0, tiled=True),
        lax.all_gather(output_weight, ("dp", "tile"), axis=0, tiled=True),
        lax.all_gather(query_bias, ("dp", "tile"), axis=0, tiled=True),
        lax.all_gather(value_bias, ("dp", "tile"), axis=0, tiled=True),
        lax.all_gather(output_bias, ("dp", "tile"), axis=0, tiled=True),
        lax.all_gather(first_gain, ("dp", "tile"), axis=0, tiled=True),
        lax.all_gather(first_shift, ("dp", "tile"), axis=0, tiled=True),
    )


def feed_weights(inner_weight, inner_bias, outer_weight, outer_bias, second_gain, second_shift):
    return (
        lax.all_gather(inner_weight, ("dp", "tile"), axis=0, tiled=True),
        lax.all_gather(inner_bias, ("dp", "tile"), axis=0, tiled=True),
        lax.all_gather(outer_weight, ("dp", "tile"), axis=0, tiled=True),
        lax.all_gather(outer_bias, ("dp", "tile"), axis=0, tiled=True),
        lax.all_gather(second_gain, ("dp", "tile"), axis=0, tiled=True),
        lax.all_gather(second_shift, ("dp", "tile"), axis=0, tiled=True),
    )


def shards(
    layer_input,
    segment_ids,
    pad_mask,
    pair_slots,
    result_cotangent,
    query_weight,
    key_weight,
    value_weight,
    output_weight,
    query_bias,
    value_bias,
    output_bias,
    first_gain,
    first_shift,
    inner_weight,
    inner_bias,
    outer_weight,
    outer_bias,
    second_gain,
    second_shift,
):
    pair_heads = HEADS // 2
    valid = pad_mask == 1
    (
        query_full,
        key_full,
        value_full,
        output_full,
        query_offset,
        value_offset,
        output_offset,
        gain_first,
        shift_first,
    ) = attention_weights(
        query_weight,
        key_weight,
        value_weight,
        output_weight,
        query_bias,
        value_bias,
        output_bias,
        first_gain,
        first_shift,
    )
    queries = (
        jnp.dot(layer_input, query_full, preferred_element_type=jnp.float32)
        + query_offset.astype(jnp.float32)
    ).astype(jnp.bfloat16)
    key_rows = jnp.dot(layer_input, key_full, preferred_element_type=jnp.float32).astype(
        jnp.bfloat16
    )
    value_rows = (
        jnp.dot(layer_input, value_full, preferred_element_type=jnp.float32)
        + value_offset.astype(jnp.float32)
    ).astype(jnp.bfloat16)
    query_pairs = to_pairs(queries, pair_heads)
    key_pairs = to_pairs(key_rows, pair_heads)
    value_pairs = to_pairs(value_rows, pair_heads)
    mixed_pairs, log_totals = attend_forward(
        query_pairs, key_pairs, value_pairs, segment_ids, valid
    )
    mixed = from_pairs(mixed_pairs)
    branch = jnp.dot(mixed, output_full, preferred_element_type=jnp.float32) + output_offset.astype(
        jnp.float32
    )
    hidden, first_back = jax.vjp(
        layer_norm,
        layer_input.astype(jnp.float32) + branch,
        gain_first.astype(jnp.float32),
        shift_first.astype(jnp.float32),
    )
    hidden_low = hidden.astype(jnp.bfloat16)
    inner_full, inner_offset, outer_full, outer_offset, gain_second, shift_second = feed_weights(
        inner_weight, inner_bias, outer_weight, outer_bias, second_gain, second_shift
    )
    inner = jnp.dot(
        hidden_low, inner_full, preferred_element_type=jnp.float32
    ) + inner_offset.astype(jnp.float32)
    active, gelu_back = jax.vjp(exact_gelu, inner)
    active_low = active.astype(jnp.bfloat16)
    outer = jnp.dot(
        active_low, outer_full, preferred_element_type=jnp.float32
    ) + outer_offset.astype(jnp.float32)
    result, second_back = jax.vjp(
        layer_norm,
        hidden + outer,
        gain_second.astype(jnp.float32),
        shift_second.astype(jnp.float32),
    )
    slots = pair_slots.shape[0]
    member = (
        (segment_ids[None, :] == jnp.arange(slots, dtype=jnp.int32)[:, None]) & valid[None, :]
    ).astype(jnp.float32)
    counts = jnp.sum(member, axis=1, keepdims=True)
    pooled = jnp.dot(member, result, precision=HIGH) / counts
    group = lax.all_gather(pooled.astype(jnp.bfloat16), "tile", axis=0, tiled=True).astype(
        pooled.dtype
    )
    numbers = jnp.arange(group.shape[0], dtype=jnp.int32)[None, :]
    choose_anchor = (pair_slots[:, 0:1] == numbers).astype(jnp.float32)
    choose_positive = (pair_slots[:, 1:2] == numbers).astype(jnp.float32)
    anchors = jnp.dot(choose_anchor, group, precision=HIGH)
    positives = jnp.dot(choose_positive, group, precision=HIGH)
    tile_count = lax.axis_size("tile")
    dp_count = lax.axis_size("dp")
    part = slots // tile_count
    tile_index = lax.axis_index("tile")
    own_half = lax.dynamic_slice_in_dim(positives, tile_index * part, part, 0)
    columns = lax.all_gather(own_half, "dp", axis=0, tiled=True)
    widths = (D, D * 2 // 3, D // 3, D // 6, D // 12)
    kept = []
    sims = []
    diags = []
    for cut in widths:
        anchor_unit, anchor_back = jax.vjp(partial(unit_rows, width=cut), anchors)
        positive_unit, positive_back = jax.vjp(partial(unit_rows, width=cut), positives)
        column_unit, column_back = jax.vjp(partial(unit_rows, width=cut), columns)
        kept.append(
            (anchor_unit, anchor_back, positive_unit, positive_back, column_unit, column_back)
        )
        sims.append(jnp.dot(anchor_unit, column_unit.T, precision=HIGH) * INV_TEMP)
        diags.append(jnp.sum(anchor_unit * positive_unit, axis=1) * INV_TEMP)
    sims = jnp.stack(sims)
    diags = jnp.stack(diags)
    shifted = jnp.exp(sims - INV_TEMP)
    row_total = lax.psum(jnp.sum(shifted, axis=2), "tile")
    column_total = lax.psum(jnp.sum(shifted, axis=1), "dp")
    row_log = INV_TEMP + jnp.log(row_total)
    column_log = INV_TEMP + jnp.log(column_total)
    local_terms = (
        0.5 * jnp.sum(row_log, axis=1) / tile_count
        + 0.5 * jnp.sum(column_log, axis=1) / dp_count
        - jnp.sum(diags, axis=1) / tile_count
    )
    dim_losses = lax.psum(local_terms, ("dp", "tile")) / (slots * dp_count)
    total_loss = jnp.sum(dim_losses)
    sim_grad = 0.5 * (jnp.exp(sims - row_log[:, :, None]) + jnp.exp(sims - column_log[:, None, :]))
    share = INV_TEMP / tile_count
    anchor_grad = jnp.zeros_like(anchors)
    positive_grad = jnp.zeros_like(positives)
    column_grad = jnp.zeros_like(columns)
    for index in range(len(widths)):
        anchor_unit, anchor_back, positive_unit, positive_back, column_unit, column_back = kept[
            index
        ]
        anchor_unit_grad = (
            jnp.dot(sim_grad[index], column_unit, precision=HIGH) * INV_TEMP - share * positive_unit
        )
        positive_unit_grad = -share * anchor_unit
        column_unit_grad = column_sum_exact(sim_grad[index], anchor_unit) * INV_TEMP
        anchor_grad = anchor_grad + anchor_back(anchor_unit_grad)[0]
        positive_grad = positive_grad + positive_back(positive_unit_grad)[0]
        column_grad = column_grad + column_back(column_unit_grad)[0]
    own_grad = lax.psum_scatter(column_grad, "dp", scatter_dimension=0, tiled=True)
    positive_grad = positive_grad + lax.dynamic_update_slice_in_dim(
        jnp.zeros_like(positive_grad), own_grad, tile_index * part, 0
    )
    group_grad = column_sum_exact(choose_anchor, anchor_grad) + column_sum_exact(
        choose_positive, positive_grad
    )
    pooled_grad = lax.psum_scatter(
        group_grad.astype(jnp.bfloat16), "tile", scatter_dimension=0, tiled=True
    ).astype(jnp.float32)
    result_grad = result_cotangent.astype(jnp.float32) + column_sum_exact(
        member, pooled_grad / counts
    )
    held = lax.optimization_barrier(
        (result_grad, inner_weight, inner_bias, outer_weight, outer_bias, second_gain, second_shift)
    )
    result_grad = held[0]
    inner_full, inner_offset, outer_full, outer_offset, gain_second, shift_second = feed_weights(
        held[1], held[2], held[3], held[4], held[5], held[6]
    )
    norm_grad, second_gain_grad, second_shift_grad = second_back(result_grad)
    outer_grad = norm_grad.astype(jnp.bfloat16)
    outer_weight_grad = column_sum(active_low, outer_grad)
    outer_bias_grad = jnp.sum(outer_grad, axis=0, dtype=jnp.float32)
    inner_grad = gelu_back(against(outer_grad, outer_full))[0].astype(jnp.bfloat16)
    inner_weight_grad = column_sum(hidden_low, inner_grad)
    inner_bias_grad = jnp.sum(inner_grad, axis=0, dtype=jnp.float32)
    hidden_grad = norm_grad + against(inner_grad, inner_full)
    (
        inner_weight_shard,
        inner_bias_shard,
        outer_weight_shard,
        outer_bias_shard,
        second_gain_shard,
        second_shift_shard,
    ) = (
        lax.psum_scatter(inner_weight_grad, ("dp", "tile"), scatter_dimension=0, tiled=True),
        lax.psum_scatter(inner_bias_grad, ("dp", "tile"), scatter_dimension=0, tiled=True),
        lax.psum_scatter(outer_weight_grad, ("dp", "tile"), scatter_dimension=0, tiled=True),
        lax.psum_scatter(outer_bias_grad, ("dp", "tile"), scatter_dimension=0, tiled=True),
        lax.psum_scatter(second_gain_grad, ("dp", "tile"), scatter_dimension=0, tiled=True),
        lax.psum_scatter(second_shift_grad, ("dp", "tile"), scatter_dimension=0, tiled=True),
    )
    held = lax.optimization_barrier(
        (
            hidden_grad,
            query_weight,
            key_weight,
            value_weight,
            output_weight,
            query_bias,
            value_bias,
            output_bias,
            first_gain,
            first_shift,
        )
    )
    hidden_grad = held[0]
    (
        query_full,
        key_full,
        value_full,
        output_full,
        query_offset,
        value_offset,
        output_offset,
        gain_first,
        shift_first,
    ) = attention_weights(
        held[1], held[2], held[3], held[4], held[5], held[6], held[7], held[8], held[9]
    )
    residual_grad, first_gain_grad, first_shift_grad = first_back(hidden_grad)
    branch_grad = residual_grad.astype(jnp.bfloat16)
    output_weight_grad = column_sum(mixed, branch_grad)
    output_bias_grad = jnp.sum(branch_grad, axis=0, dtype=jnp.float32)
    mixed_grad = against(branch_grad, output_full).astype(jnp.bfloat16)
    query_grad_pairs, key_grad_pairs, value_grad_pairs = attend_backward(
        query_pairs,
        key_pairs,
        value_pairs,
        to_pairs(mixed_grad, pair_heads),
        log_totals,
        segment_ids,
        valid,
    )
    query_grad = from_pairs(query_grad_pairs)
    key_grad = from_pairs(key_grad_pairs)
    value_grad = from_pairs(value_grad_pairs)
    query_weight_grad = column_sum(layer_input, query_grad)
    key_weight_grad = column_sum(layer_input, key_grad)
    value_weight_grad = column_sum(layer_input, value_grad)
    query_bias_grad = jnp.sum(query_grad, axis=0, dtype=jnp.float32)
    value_bias_grad = jnp.sum(value_grad, axis=0, dtype=jnp.float32)
    input_grad = (
        residual_grad
        + against(query_grad, query_full)
        + against(key_grad, key_full)
        + against(value_grad, value_full)
    )
    (
        query_weight_shard,
        key_weight_shard,
        value_weight_shard,
        output_weight_shard,
        query_bias_shard,
        value_bias_shard,
        output_bias_shard,
        first_gain_shard,
        first_shift_shard,
    ) = (
        lax.psum_scatter(query_weight_grad, ("dp", "tile"), scatter_dimension=0, tiled=True),
        lax.psum_scatter(key_weight_grad, ("dp", "tile"), scatter_dimension=0, tiled=True),
        lax.psum_scatter(value_weight_grad, ("dp", "tile"), scatter_dimension=0, tiled=True),
        lax.psum_scatter(output_weight_grad, ("dp", "tile"), scatter_dimension=0, tiled=True),
        lax.psum_scatter(query_bias_grad, ("dp", "tile"), scatter_dimension=0, tiled=True),
        lax.psum_scatter(value_bias_grad, ("dp", "tile"), scatter_dimension=0, tiled=True),
        lax.psum_scatter(output_bias_grad, ("dp", "tile"), scatter_dimension=0, tiled=True),
        lax.psum_scatter(first_gain_grad, ("dp", "tile"), scatter_dimension=0, tiled=True),
        lax.psum_scatter(first_shift_grad, ("dp", "tile"), scatter_dimension=0, tiled=True),
    )
    return (
        total_loss,
        dim_losses,
        result.astype(jnp.bfloat16),
        input_grad,
        query_weight_shard,
        key_weight_shard,
        value_weight_shard,
        output_weight_shard,
        query_bias_shard,
        value_bias_shard,
        output_bias_shard,
        first_gain_shard,
        first_shift_shard,
        inner_weight_shard,
        inner_bias_shard,
        outer_weight_shard,
        outer_bias_shard,
        second_gain_shard,
        second_shift_shard,
    )


def solution(mesh):
    return jax.shard_map(
        shards,
        mesh=mesh,
        in_specs=(
            P(("dp", "tile"), None),
            P(("dp", "tile")),
            P(("dp", "tile")),
            P("dp", None),
            P(("dp", "tile"), None),
            P(("dp", "tile"), None),
            P(("dp", "tile"), None),
            P(("dp", "tile"), None),
            P(("dp", "tile"), None),
            P(("dp", "tile")),
            P(("dp", "tile")),
            P(("dp", "tile")),
            P(("dp", "tile")),
            P(("dp", "tile")),
            P(("dp", "tile"), None),
            P(("dp", "tile")),
            P(("dp", "tile"), None),
            P(("dp", "tile")),
            P(("dp", "tile")),
            P(("dp", "tile")),
        ),
        out_specs=(
            P(),
            P(),
            P(("dp", "tile"), None),
            P(("dp", "tile"), None),
            P(("dp", "tile"), None),
            P(("dp", "tile"), None),
            P(("dp", "tile"), None),
            P(("dp", "tile"), None),
            P(("dp", "tile")),
            P(("dp", "tile")),
            P(("dp", "tile")),
            P(("dp", "tile")),
            P(("dp", "tile")),
            P(("dp", "tile"), None),
            P(("dp", "tile")),
            P(("dp", "tile"), None),
            P(("dp", "tile")),
            P(("dp", "tile")),
            P(("dp", "tile")),
        ),
        check_vma=False,
    )
```

profile of v0, /device:TPU:0, one launch (start us, length us, event | category | flops | bytes accessed | tf_op | source)
XLA Modules:
  0.0 1731.3 jit_solution(4277878657754773702)
XLA Ops:
  18.8 42.4 %all-reduce.35 = (bf16[768]{0:T(1024)(128)(2,1)S(1)}, bf16[768]{0:T(1024)(128)(2,1)S(1)}, bf16[768]{0:T(1024)(128)(2,1)S(1)}, bf16[768]{0:T(1024)(128)(2,1)S(1)}...) all-reduce(bf16[768]{0:T(1024)(128)(2,1)S(1)} %dynamic-update-slice, ...), channel_id=1, replica_groups=mesh['dp'=16,'tile'=2] {'dp','tile'}, use_global_device_ids=true, to_apply=%add.12 | all-reduce | flops 9216 | bytes 36864
  73.5 5.4 add_convert_fusion.2
  83.3 40.8 %all-gather.17.cloned.1.call-done = bf16[768,768]{1,0:T(8,128)(2,1)} async-done(((bf16[24,768]{1,0:T(8,128)(2,1)}), bf16[768,768]{1,0:T(8,128)(2,1)}) %all-gather.17.cloned.1.call-update) | async-done | bytes 1179664 | tf_op jit(solution)/shard_map/all_gather | solution.py:187
  124.0 5.4 convolution_convert_fusion.1
  129.4 50.5 %all-gather.19.cloned.1.call-done = bf16[768,768]{1,0:T(8,128)(2,1)} async-done(((bf16[24,768]{1,0:T(8,128)(2,1)}), bf16[768,768]{1,0:T(8,128)(2,1)}) %all-gather.19.cloned.1.call-update) | async-done | bytes 1179664 | tf_op jit(solution)/shard_map/all_gather | solution.py:188
  179.9 5.5 add_convert_fusion.1
  185.4 137.3 %while.54 = (s32[]{:T(128)}, bf16[6,3,512,128]{3,2,1,0:T(8,128)(2,1)}, f32[6,3,2,512,1]{3,2,1,4,0:T(2,128)}, bf16[6,1536,128]{2,1,0:T(8,128)(2,1)}, bf16[6,1536,...) while((s32[]{:T(128)}, ...), condition=%wide.region_5.6_spmd, body=%wide.region_0.5_spmd.sunk | while | flops 423164928 | bytes 27859792 | solution.py:102
  187.6 19.0 %while.57 = (s32[]{:T(128)}, bf16[3,512,128]{1,2,0:T(8,128)(2,1)S(1)}, f32[3,2,512,1]{2,1,3,0:T(2,128)S(1)}, s32[3,512]{1,0:T(4,128)S(1)}, s32[1536]{0:T(1024)S(...) while((s32[]{:T(128)}, ...), condition=%wide.region_4.4_spmd, body=%wide.region_1.3_spmd.sunk | while | flops 423164928 | bytes 23901812 | solution.py:98
  210.5 19.0 %while.57 = (s32[]{:T(128)}, bf16[3,512,128]{1,2,0:T(8,128)(2,1)S(1)}, f32[3,2,512,1]{2,1,3,0:T(2,128)S(1)}, s32[3,512]{1,0:T(4,128)S(1)}, s32[1536]{0:T(1024)S(...) while((s32[]{:T(128)}, ...), condition=%wide.region_4.4_spmd, body=%wide.region_1.3_spmd.sunk | while | flops 423164928 | bytes 23901812 | solution.py:98
  233.4 19.0 %while.57 = (s32[]{:T(128)}, bf16[3,512,128]{1,2,0:T(8,128)(2,1)S(1)}, f32[3,2,512,1]{2,1,3,0:T(2,128)S(1)}, s32[3,512]{1,0:T(4,128)S(1)}, s32[1536]{0:T(1024)S(...) while((s32[]{:T(128)}, ...), condition=%wide.region_4.4_spmd, body=%wide.region_1.3_spmd.sunk | while | flops 423164928 | bytes 23901812 | solution.py:98
  256.2 19.0 %while.57 = (s32[]{:T(128)}, bf16[3,512,128]{1,2,0:T(8,128)(2,1)S(1)}, f32[3,2,512,1]{2,1,3,0:T(2,128)S(1)}, s32[3,512]{1,0:T(4,128)S(1)}, s32[1536]{0:T(1024)S(...) while((s32[]{:T(128)}, ...), condition=%wide.region_4.4_spmd, body=%wide.region_1.3_spmd.sunk | while | flops 423164928 | bytes 23901812 | solution.py:98
  279.1 19.0 %while.57 = (s32[]{:T(128)}, bf16[3,512,128]{1,2,0:T(8,128)(2,1)S(1)}, f32[3,2,512,1]{2,1,3,0:T(2,128)S(1)}, s32[3,512]{1,0:T(4,128)S(1)}, s32[1536]{0:T(1024)S(...) while((s32[]{:T(128)}, ...), condition=%wide.region_4.4_spmd, body=%wide.region_1.3_spmd.sunk | while | flops 423164928 | bytes 23901812 | solution.py:98
  302.0 19.0 %while.57 = (s32[]{:T(128)}, bf16[3,512,128]{1,2,0:T(8,128)(2,1)S(1)}, f32[3,2,512,1]{2,1,3,0:T(2,128)S(1)}, s32[3,512]{1,0:T(4,128)S(1)}, s32[1536]{0:T(1024)S(...) while((s32[]{:T(128)}, ...), condition=%wide.region_4.4_spmd, body=%wide.region_1.3_spmd.sunk | while | flops 423164928 | bytes 23901812 | solution.py:98
  325.8 5.4 fusion.152
  334.2 49.6 %multiply_convert_fusion.1 = (bf16[1536,3072]{1,0:T(8,128)(2,1)}, f32[1536,3072]{1,0:T(8,128)}, f32[1536,3072]{1,0:T(8,128)}) fusion(f32[3072]{0:T(1024)S(1)} %copy-done.48, bf16[768,3072]{1,0:T(8,128)(2,1)} %all-gather.23.cloned.1.call-done, bf16[1536,768]{0,1:T(8,128)(2,1)S(1)} %fusion.147.clone.4), kind=kOutput, calls=%fused_computation.49 | convolution fusion | flops 7559184384 | bytes 54276096 | tf_op jit(solution)/shard_map/dot_general | solution.py:285
  383.8 13.5 fusion.153
  404.4 40.7 %all-gather.1 = f32[16,6,768]{2,1,0:T(8,128)S(1)} all-gather(f32[1,6,768]{2,1,0:T(8,128)S(1)} %dynamic-slice_bitcast_fusion.2), channel_id=1, replica_groups=mesh['dp'=16,'tile'=2] {'dp'}, dimensions={0}, use_global_device_ids=true | all-gather | bytes 313344 | tf_op jit(solution)/shard_map/all_gather | solution.py:318
  450.7 36.5 %psum.22 = f32[5,96]{1,0:T(8,128)S(1)} all-reduce(f32[5,96]{1,0:T(8,128)S(1)} %get-tuple-element.512), channel_id=1, replica_groups=mesh['dp'=16,'tile'=2] {'dp'}, use_global_device_ids=true, to_apply=%region_25.26 | all-reduce | flops 480 | bytes 3840 | tf_op jit(solution)/shard_map/psum | solution.py:336
  490.7 42.4 %fusion = f32[8,768]{1,0:T(8,128)S(1)} fusion(f32[96,768]{1,0:T(8,128)S(1)} %fusion.55), kind=kCustom, calls=%all-reduce-scatter | all-reduce-scatter fusion | flops 98305 | bytes 320000
  560.3 5.2 multiply_reduce_fusion.1
  565.6 5.9 fusion.150
  574.7 49.4 %all-gather.27.cloned.1.call-done = bf16[3072,768]{1,0:T(8,128)(2,1)} async-done(((bf16[96,768]{1,0:T(8,128)(2,1)}), bf16[3072,768]{1,0:T(8,128)(2,1)}) %all-gather.27.cloned.1.call-update) | async-done | bytes 4718608 | tf_op jit(solution)/shard_map/all_gather | solution.py:202
  624.1 23.6 %convert_reduce_fusion = (f32[3072]{0:T(1024)}, bf16[1536,3072]{1,0:T(8,128)(2,1)}) fusion(f32[1536,3072]{1,0:T(8,128)} %get-tuple-element.627, bf16[1536,768]{0,1:T(8,128)(2,1)S(1)} %get-tuple-element.619, bf16[3072,768]{1,0:T(8,128)(2,1)} %all-gather.27.cloned.1.call-done, f32[1536,3072]{1,0:T(8,128)} %get-tuple-element.675, f32[3072]{0:T(1024)S(1)} %copy-done.48), kind=kOutput, calls=%fused_computation.47 | convolution fusion | flops 7327970304 | bytes 54288384 | tf_op jit(solution)/shard_map/dot_general | solution.py:49
  647.6 41.8 %all-gather.29.cloned.1.call-done = bf16[768,3072]{1,0:T(8,128)(2,1)} async-done(((bf16[24,3072]{1,0:T(8,128)(2,1)}), bf16[768,3072]{1,0:T(8,128)(2,1)}) %all-gather.29.cloned.1.call-update) | async-done | bytes 4718608 | tf_op jit(solution)/shard_map/all_gather | solution.py:200
  689.5 14.2 add_add_fusion.5
  705.9 5.2 multiply_reduce_fusion.2
  711.1 5.0 fusion.149
  724.6 12.3 fusion.156
  737.2 19.6 %all-gather.31.cloned.1.call-done = bf16[768,768]{1,0:T(8,128)(2,1)} async-done(((bf16[24,768]{1,0:T(8,128)(2,1)}), bf16[768,768]{1,0:T(8,128)(2,1)}) %all-gather.31.cloned.1.call-update) | async-done | bytes 1179664 | tf_op jit(solution)/shard_map/all_gather | solution.py:189
  763.2 502.7 %while.56 = (s32[]{:T(128)}, bf16[6,1536,128]{1,2,0:T(8,128)(2,1)}, bf16[6,1536,128]{1,2,0:T(8,128)(2,1)}, bf16[6,1536,128]{1,2,0:T(8,128)(2,1)}, bf16[6,1536,12...) while((s32[]{:T(128)}, bf16[6,1536,128]{1,2,0:T(8,128)(2,1)}, ...), condition=%wide.region_65.66_spmd, body=%wide.region_61.65_spmd.sunk | while | flops 1023867904 | bytes 118648648 | solution.py:171
  768.1 73.5 %while.58 = (s32[]{:T(128)}, f32[1536,2,64]{0,2,1:T(8,128)}, f32[1536,2,64]{0,2,1:T(8,128)}, bf16[3,512,128]{2,1,0:T(8,128)(2,1)}, bf16[3,512,128]{2,1,0:T(8,128...) while((s32[]{:T(128)}, f32[1536,2,64]{0,2,1:T(8,128)}, ...), condition=%wide.region_64.64_spmd.clone, body=%wide.region_62.63_spmd.clone.sunk | while | flops 1023474688 | bytes 109972000 | solution.py:155
  773.4 4.9 multiply_reduce_fusion.43
  797.5 5.0 multiply_reduce_fusion.43
  822.3 4.9 multiply_reduce_fusion.43
  851.7 73.3 %while.58 = (s32[]{:T(128)}, f32[1536,2,64]{0,2,1:T(8,128)}, f32[1536,2,64]{0,2,1:T(8,128)}, bf16[3,512,128]{2,1,0:T(8,128)(2,1)}, bf16[3,512,128]{2,1,0:T(8,128...) while((s32[]{:T(128)}, f32[1536,2,64]{0,2,1:T(8,128)}, ...), condition=%wide.region_64.64_spmd.clone, body=%wide.region_62.63_spmd.clone.sunk | while | flops 1023474688 | bytes 109972000 | solution.py:155
  857.0 4.9 multiply_reduce_fusion.43
  881.1 4.9 multiply_reduce_fusion.43
  935.2 73.6 %while.58 = (s32[]{:T(128)}, f32[1536,2,64]{0,2,1:T(8,128)}, f32[1536,2,64]{0,2,1:T(8,128)}, bf16[3,512,128]{2,1,0:T(8,128)(2,1)}, bf16[3,512,128]{2,1,0:T(8,128...) while((s32[]{:T(128)}, f32[1536,2,64]{0,2,1:T(8,128)}, ...), condition=%wide.region_64.64_spmd.clone, body=%wide.region_62.63_spmd.clone.sunk | while | flops 1023474688 | bytes 109972000 | solution.py:155
  940.5 5.0 multiply_reduce_fusion.43
  964.8 5.0 multiply_reduce_fusion.43
  989.5 4.9 multiply_reduce_fusion.43
  1018.9 74.5 %while.58 = (s32[]{:T(128)}, f32[1536,2,64]{0,2,1:T(8,128)}, f32[1536,2,64]{0,2,1:T(8,128)}, bf16[3,512,128]{2,1,0:T(8,128)(2,1)}, bf16[3,512,128]{2,1,0:T(8,128...) while((s32[]{:T(128)}, f32[1536,2,64]{0,2,1:T(8,128)}, ...), condition=%wide.region_64.64_spmd.clone, body=%wide.region_62.63_spmd.clone.sunk | while | flops 1023474688 | bytes 109972000 | solution.py:155
  1024.3 4.9 multiply_reduce_fusion.43
  1048.6 5.2 multiply_reduce_fusion.43
  1063.5 5.0 fusion.242
  1073.8 5.2 multiply_reduce_fusion.43
  1103.6 73.6 %while.58 = (s32[]{:T(128)}, f32[1536,2,64]{0,2,1:T(8,128)}, f32[1536,2,64]{0,2,1:T(8,128)}, bf16[3,512,128]{2,1,0:T(8,128)(2,1)}, bf16[3,512,128]{2,1,0:T(8,128...) while((s32[]{:T(128)}, f32[1536,2,64]{0,2,1:T(8,128)}, ...), condition=%wide.region_64.64_spmd.clone, body=%wide.region_62.63_spmd.clone.sunk | while | flops 1023474688 | bytes 109972000 | solution.py:155
  1108.9 5.1 multiply_reduce_fusion.43
  1157.9 4.9 multiply_reduce_fusion.43
  1187.2 73.3 %while.58 = (s32[]{:T(128)}, f32[1536,2,64]{0,2,1:T(8,128)}, f32[1536,2,64]{0,2,1:T(8,128)}, bf16[3,512,128]{2,1,0:T(8,128)(2,1)}, bf16[3,512,128]{2,1,0:T(8,128...) while((s32[]{:T(128)}, f32[1536,2,64]{0,2,1:T(8,128)}, ...), condition=%wide.region_64.64_spmd.clone, body=%wide.region_62.63_spmd.clone.sunk | while | flops 1023474688 | bytes 109972000 | solution.py:155
  1192.6 4.9 multiply_reduce_fusion.43
  1216.7 4.9 multiply_reduce_fusion.43
  1265.9 5.8 convolution_bitcast_fusion.2
  1275.0 5.1 convolution_bitcast_fusion.1
  1283.6 5.1 convolution_bitcast_fusion
  1292.0 13.9 fusion.144
  1314.6 40.1 %all-reduce.34 = (f32[5]{0:T(128)S(1)}, f32[768]{0:T(1024)S(1)}, f32[768]{0:T(1024)S(1)}, f32[768]{0:T(1024)S(1)}, f32[768]{0:T(1024)S(1)}, /*index=5*/f32[768]{...) all-reduce(f32[5]{0:T(128)S(1)} %multiply_subtract_fusion, ...), channel_id=1, replica_groups=mesh['dp'=16,'tile'=2] {'dp','tile'}, use_global_device_ids=true, to_apply=%region_38.39 | all-reduce | flops 9221 | bytes 73768 | tf_op jit(solution)/shard_map/psum | solution.py:344
  1354.8 5.5 fusion.157
  1360.3 6.4 fusion.158
  1366.7 9.8 add_add_fusion.2
  1376.5 6.0 copy.129
  1388.9 89.5 %reduce-scatter.25.cloned.1.call-done = f32[24,768]{1,0:T(8,128)} async-done(((f32[768,768]{1,0:T(8,128)}), f32[24,768]{1,0:T(8,128)}) %reduce-scatter.25.cloned.1.call-update) | async-done | bytes 73744
  1478.4 103.8 %reduce-scatter.27.cloned.1.call-done = f32[24,768]{1,0:T(8,128)} async-done(((f32[768,768]{1,0:T(8,128)}), f32[24,768]{1,0:T(8,128)}) %reduce-scatter.27.cloned.1.call-update) | async-done | bytes 73744
  1582.1 141.9 %reduce-scatter.19.cloned.1.call-done = f32[24,3072]{1,0:T(8,128)} async-done(((f32[768,3072]{1,0:T(8,128)}), f32[24,3072]{1,0:T(8,128)}) %reduce-scatter.19.cloned.1.call-update) | async-done | bytes 294928 | tf_op jit(solution)/shard_map/reduce_scatter | solution.py:399
  (1335 shorter events, 676.4 us)
Async XLA Ops:
  7.2 65.1 %copy-start.61 = (u32[32]{0:T(128)S(1)}, u32[32]{0:T(128)}, u32[]{:S(2)}) copy-start(u32[32]{0:T(128)} %constant.297) | copy-start | bytes 388
  7.2 63.9 %copy-start.12 = (s32[1536]{0:T(1024)S(1)}, s32[1536]{0:T(1024)}, u32[]{:S(2)}) copy-start(s32[1536]{0:T(1024)} %param.29) | copy-start | bytes 18436
  7.2 64.5 %copy-start.57 = (s32[12,2]{0,1:T(2,128)S(1)}, s32[12,2]{0,1:T(2,128)}, u32[]{:S(2)}) copy-start(s32[12,2]{0,1:T(2,128)} %param.31) | copy-start | bytes 292
  7.2 66.3 %all-gather.15.cloned.1.call-start = ((), (), s32[]{:S(2)}) async-start(), calls=%async_computation.6 | async-start | bytes 1216512 | tf_op jit(solution)/shard_map/all_gather | solution.py:186
  8.0 116.1 %all-gather.17.cloned.1.call-start = ((), (), s32[]{:S(2)}) async-start(), calls=%async_computation.7 | async-start | bytes 1216512 | tf_op jit(solution)/shard_map/all_gather | solution.py:187
  8.7 171.2 %all-gather.19.cloned.1.call-start = ((), (), s32[]{:S(2)}) async-start(), calls=%async_computation.8 | async-start | bytes 1216512 | tf_op jit(solution)/shard_map/all_gather | solution.py:188
  9.4 316.3 %all-gather.21.cloned.1.call-start = ((), (), s32[]{:S(2)}) async-start(), calls=%async_computation.9 | async-start | bytes 1216512 | tf_op jit(solution)/shard_map/all_gather | solution.py:189
  10.0 324.2 %all-gather.23.cloned.1.call-start = ((), (), s32[]{:S(2)}) async-start(), calls=%async_computation.10 | async-start | bytes 4866048 | tf_op jit(solution)/shard_map/all_gather | solution.py:200
  10.6 373.2 %all-gather.25.cloned.1.call-start = ((), (), s32[]{:S(2)}) async-start(), calls=%async_computation.11 | async-start | bytes 4866048 | tf_op jit(solution)/shard_map/all_gather | solution.py:202
  11.2 612.9 %all-gather.27.cloned.1.call-start = ((), (), s32[]{:S(2)}) async-start(), calls=%async_computation.12 | async-start | bytes 4866048 | tf_op jit(solution)/shard_map/all_gather | solution.py:202
  331.3 379.8 %copy-start.28 = (f32[1536]{0:T(1024)}, f32[1536]{0:T(1024)S(1)}, u32[]{:S(2)}) copy-start(f32[1536]{0:T(1024)S(1)} %broadcast_multiply_fusion.1) | copy-start | bytes 18436
  331.8 52.0 %copy-start.34 = (f32[1536]{0:T(1024)}, f32[1536]{0:T(1024)S(1)}, u32[]{:S(2)}) copy-start(f32[1536]{0:T(1024)S(1)} %multiply_reduce_fusion.6) | copy-start | bytes 18436
  333.4 377.7 %copy-start.30 = (f32[1536]{0:T(1024)}, f32[1536]{0:T(1024)S(1)}, u32[]{:S(2)}) copy-start(f32[1536]{0:T(1024)S(1)} %fusion.130) | copy-start | bytes 18436
  334.2 49.6 %copy-start.52 = (f32[768]{0:T(1024)S(1)}, f32[768]{0:T(1024)}, u32[]{:S(2)}) copy-start(f32[768]{0:T(1024)} %convert_element_type.134) | copy-start | bytes 9220
  445.2 105.6 %copy-start.60 = (u32[32]{0:T(128)S(1)}, u32[32]{0:T(128)}, u32[]{:S(2)}) copy-start(u32[32]{0:T(128)} %constant.301) | copy-start | bytes 388
  533.2 11.4 collective-permute-start
  535.5 9.1 collective-permute-start.1
  536.8 7.8 collective-permute-start.2
  538.1 6.5 collective-permute-start.3
  548.5 6.4 collective-permute-start.4
  559.5 130.0 %all-gather.29.cloned.1.call-start = ((), (), s32[]{:S(2)}) async-start(), calls=%async_computation.13 | async-start | bytes 4866048 | tf_op jit(solution)/shard_map/all_gather | solution.py:200
  560.3 196.5 %all-gather.31.cloned.1.call-start = ((), (), s32[]{:S(2)}) async-start(), calls=%async_computation.14 | async-start | bytes 1216512 | tf_op jit(solution)/shard_map/all_gather | solution.py:189
  703.7 651.0 %all-gather.33.cloned.1.call-start = ((), (), s32[]{:S(2)}) async-start(), calls=%async_computation.15 | async-start | bytes 1216512 | tf_op jit(solution)/shard_map/all_gather | solution.py:186
  704.3 656.0 %all-gather.35.cloned.1.call-start = ((), (), s32[]{:S(2)}) async-start(), calls=%async_computation.16 | async-start | bytes 1216512 | tf_op jit(solution)/shard_map/all_gather | solution.py:187
  705.1 661.6 %all-gather.37.cloned.1.call-start = ((), (), s32[]{:S(2)}) async-start(), calls=%async_computation.17 | async-start | bytes 1216512 | tf_op jit(solution)/shard_map/all_gather | solution.py:188
  705.7 683.2 %reduce-scatter.17.cloned.1.call-start = ((), (), s32[]{:S(2)}) async-start(), calls=%async_computation.18 | async-start | bytes 2433024 | tf_op jit(solution)/shard_map/reduce_scatter | solution.py:476
  724.5 664.4 %reduce-scatter.21.cloned.1.call-start = ((), (), s32[]{:S(2)}) async-start(), calls=%async_computation.20 | async-start | bytes 9732096 | tf_op jit(solution)/shard_map/reduce_scatter | solution.py:401
  736.9 652.0 %reduce-scatter.23.cloned.1.call-start = ((), (), s32[]{:S(2)}) async-start(), calls=%async_computation.21 | async-start | bytes 2433024
  792.1 10.4 copy-start.3
  792.2 10.4 copy-start.6
  792.2 10.4 copy-start.8
  792.2 10.4 copy-start.25
  816.9 10.3 copy-start.3
  816.9 10.3 copy-start.6
  817.0 10.3 copy-start.8
  817.0 10.3 copy-start.25
  935.2 10.3 copy-start.3
  935.2 10.3 copy-start.6
  935.2 10.3 copy-start.8
  935.2 10.3 copy-start.25
  959.4 10.3 copy-start.3
  959.5 10.3 copy-start.6
  959.5 10.3 copy-start.8
  959.5 10.3 copy-start.25
  984.1 10.3 copy-start.3
  984.2 10.3 copy-start.6
  984.2 10.3 copy-start.8
  984.2 10.3 copy-start.25
  1043.3 10.5 copy-start.3
  1043.3 10.5 copy-start.6
  1043.3 10.5 copy-start.8
  1043.3 10.5 copy-start.25
  1068.5 10.5 copy-start.3
  1068.5 10.5 copy-start.6
  1068.5 10.5 copy-start.8
  1068.5 10.5 copy-start.25
  1103.6 10.4 copy-start.3
  1103.6 10.4 copy-start.6
  1103.6 10.4 copy-start.8
  1103.6 10.4 copy-start.25
  1274.9 203.4 %reduce-scatter.25.cloned.1.call-start = ((), (), s32[]{:S(2)}) async-start(), calls=%async_computation.22 | async-start | bytes 2433024
  1283.3 298.8 %reduce-scatter.27.cloned.1.call-start = ((), (), s32[]{:S(2)}) async-start(), calls=%async_computation.23 | async-start | bytes 2433024
  1291.9 432.1 %reduce-scatter.19.cloned.1.call-start = ((), (), s32[]{:S(2)}) async-start(), calls=%async_computation.19 | async-start | bytes 9732096 | tf_op jit(solution)/shard_map/reduce_scatter | solution.py:399
  1310.2 44.5 %copy-start.23 = (bf16[6,1536,128]{1,2,0:T(8,128)(2,1)S(1)}, bf16[6,1536,128]{1,2,0:T(8,128)(2,1)}, u32[]{:S(2)}) copy-start(bf16[6,1536,128]{1,2,0:T(8,128)(2,1)} %get-tuple-element.1240) | copy-start | bytes 7077892
  (247 other events, 1556.6 us)
Sparse Core Ops, SparseCore 0:
  11.0 56.9 all-gather.14
  70.9 53.1 all-gather.16
  126.9 52.9 all-gather.18
  182.7 53.0 all-gather.20
  238.5 62.5 all-gather.22
  303.8 62.4 all-gather.24
  559.6 64.4 all-gather.26
  627.0 62.4 all-gather.28
  703.9 52.8 all-gather.30
  759.5 52.9 all-gather.32
  815.4 53.0 all-gather.34
  871.2 52.9 all-gather.36
  930.1 97.9 reduce-scatter.16
  1035.4 134.3 reduce-scatter.20
  1275.1 98.6 reduce-scatter.22
  1380.3 98.0 reduce-scatter.24
  1484.1 97.9 reduce-scatter.26
  1589.4 134.5 reduce-scatter.18
where the time goes:
time: 1750 us; the launch traced here: 1730 us
  matrix products  592 us (34%)
  waiting for transfers between devices  543 us (31%)
  local copies, waits for them, and re-layouts  232 us (13%)
  blocking collectives  209 us (12%)
  other arithmetic  121 us (7%)
    unnamed x26, waiting for transfers between devices  199 us
    reduce_scatter x1, waiting for transfers between devices, shards(): lax.psum_scatter(inner_weight_grad, ('dp', 'tile'), scatter_dimension=0,...  142 us
    dot_general x36, matrix products, masked_scores(): jnp.einsum('qhd,khd->hqk', heads, key_heads, preferred_element_type=jnp.f...  117 us
    unnamed x3, blocking collectives  87.7 us
    dot_general x18, matrix products, per_block(): jnp.einsum('hqk,qhd->khd', probs.astype(jnp.bfloat16), grads, preferred_e...  83.7 us
    dot_general x18, matrix products, per_block(): jnp.einsum('qhd,khd->hqk', grads, value_heads, preferred_element_type=jnp...  65.6 us
    dot_general x6, matrix products, against(): lax.dot_general(grad, weight, (((1,), (1,)), ((), ())), preferred_element...  63.5 us
    all_gather x2, waiting for transfers between devices, attention_weights(): lax.all_gather(value_weight, ('dp', 'tile'), axis=0, tiled=True)  50.5 us
  transfers between devices with their start and end apart: 23, of which 8 were waited for; matrix products, arithmetic and copies ran while one was open for 49% of the time, Pallas kernels for 0%

commit v1 on v0

v1 whole, which is shorter than its diff:
```python
import functools

import jax
import jax.numpy as jnp
from jax import lax
from jax.experimental import pallas as pl
from jax.experimental.pallas import tpu as pltpu
from jax.sharding import PartitionSpec as P

D = 768
HEADS = 12
HEAD_DIM = 64
EPS_NORM = 1e-12
EPS_UNIT = 1e-06
INV_TEMP = 20.0
NEG_FILL = -1e30
HIGH = lax.Precision.HIGHEST
F32 = jnp.float32
BF = jnp.bfloat16
NT = (((1,), (1,)), ((), ()))
TN = (((0,), (0,)), ((), ()))
FWD_TILES = (512, 512, 2)
BWD_TILES = (512, 512, 2)
PAD_SLOTS = 16


def dot(a, b):
    return jnp.dot(a, b, preferred_element_type=F32)


def nt(a, b):
    return lax.dot_general(a, b, NT, preferred_element_type=F32)


def tn(a, b):
    return lax.dot_general(a, b, TN, preferred_element_type=F32)


def digits_of(count):
    digits, stride = [], 1
    while count > 1:
        radix = 4 if count % 4 == 0 else (2 if count % 2 == 0 else count)
        digits.append((stride, radix))
        stride, count = stride * radix, count // radix
    return digits


def peer(index, stride, radix, step):
    digit = index // stride % radix
    other = digit ^ step if radix in (2, 4) else (digit + step) % radix
    return index + (other - digit) * stride


def back(index, stride, radix, step):
    digit = index // stride % radix
    other = digit ^ step if radix in (2, 4) else (digit - step) % radix
    return index + (other - digit) * stride


def send_to(value, count, stride, radix, step):
    return lax.ppermute(value, "dp", [(i, peer(i, stride, radix, step)) for i in range(count)])


def swap_tile(value):
    return lax.ppermute(value, "tile", [(0, 1), (1, 0)])


def gather_pieces(shard):
    count, me = lax.axis_size("dp"), lax.axis_index("dp")
    stack, sources = shard[None], [me]
    digits = digits_of(count)[::-1]
    for level, (stride, radix) in enumerate(digits):
        stacks, origins = [stack], [sources]
        for step in range(1, radix):
            stacks.append(send_to(stack, count, stride, radix, step))
            origins.append([back(source, stride, radix, step) for source in sources])
        if level == len(digits) - 1:
            return stacks, origins
        stack, sources = jnp.concatenate(stacks, axis=0), sum(origins, [])
    return [stack], [sources]


def place_kernel(slots, *refs, sizes):
    count = len(sizes)
    pieces, out, sems = refs[:count], refs[count], refs[count + 1]
    copies, number = [], 0
    for piece, size in zip(pieces, sizes):
        for entry in range(size):
            copies.append(pltpu.make_async_copy(piece.at[entry], out.at[slots[number]], sems.at[number]))
            number += 1
    for copy in copies:
        copy.start()
    for copy in copies:
        copy.wait()


def gather_rows(shard):
    stacks, origins = gather_pieces(shard)
    tile = lax.axis_index("tile")
    others = [swap_tile(stack) for stack in stacks]
    slots = [origin * 2 + tile for group in origins for origin in group]
    slots += [origin * 2 + (1 - tile) for group in origins for origin in group]
    sizes = [stack.shape[0] for stack in stacks] * 2
    total = sum(sizes)
    placed = pl.pallas_call(
        functools.partial(place_kernel, sizes=sizes),
        out_shape=jax.ShapeDtypeStruct((total,) + shard.shape, shard.dtype),
        grid_spec=pltpu.PrefetchScalarGridSpec(
            num_scalar_prefetch=1,
            grid=(1,),
            in_specs=[pl.BlockSpec(memory_space=pl.ANY)] * len(sizes),
            out_specs=pl.BlockSpec((total,) + shard.shape, lambda i, *_: (0, 0, 0)),
            scratch_shapes=[pltpu.SemaphoreType.DMA((total,))],
        ),
        name="place_rows",
    )(jnp.stack(slots).astype(jnp.int32), *stacks, *others)
    return placed.reshape(total * shard.shape[0], shard.shape[1])


def take(value, index, axis):
    return lax.dynamic_index_in_dim(value, index, axis, keepdims=False)


def scatter_rows(partial):
    count, me = lax.axis_size("dp"), lax.axis_index("dp")
    tile = lax.axis_index("tile")
    rows = partial.shape[0] // (2 * count)
    blocks = partial.reshape(count, 2, rows, partial.shape[1])
    got = swap_tile(take(blocks, 1 - tile, 1))
    total = take(blocks, tile, 1).astype(F32) + got.astype(F32)
    for stride, radix in digits_of(count):
        total = total.astype(BF).reshape(-1, radix, rows, partial.shape[1])
        digit = me // stride % radix
        sent = []
        for step in range(1, radix):
            other = peer(me, stride, radix, step) // stride % radix
            sent.append(send_to(take(total, other, 1), count, stride, radix, step))
        total = take(total, digit, 1).astype(F32)
        for value in sent:
            total = total + value.astype(F32)
    return total.reshape(rows, partial.shape[1])


def key_ranges(segment_ids, valid, tq, tk):
    rows = segment_ids.shape[0]
    tiles = segment_ids.reshape(rows // tq, tq)
    first, last = tiles[:, 0], tiles[:, -1]
    lo = jnp.sum((segment_ids[None, :] < first[:, None]).astype(jnp.int32), axis=1)
    hi = jnp.sum(((segment_ids[None, :] <= last[:, None]) & valid[None, :]).astype(jnp.int32), axis=1)
    return lo // tk, (hi + tk - 1) // tk


def mask_codes(segment_ids, valid, slots):
    half = 64
    ids = jnp.arange(half, dtype=jnp.int32)
    code = jnp.where(valid, segment_ids, slots)
    keys = (code[:, None] == ids[None, :]).astype(BF)
    block = (segment_ids[None, :] != ids[:, None]) & (ids[:, None] <= slots)
    queries = jnp.where(block, NEG_FILL, 0.0).astype(BF)
    return keys, queries


def fwd_kernel(lo_ref, hi_ref, q_ref, k_ref, v_ref, kc_ref, qc_ref, o_ref, lse_ref, kaug, vt, *, tq, tk):
    rows = q_ref.shape[0]
    nh = q_ref.shape[1] // 64
    kc = kc_ref[...]
    k = k_ref[...]
    for h in range(nh):
        kaug[h] = jnp.concatenate([k[:, 64 * h:64 * h + 64], kc], axis=1)
    vt[...] = v_ref[...].T

    def q_step(i, _):
        q0 = pl.multiple_of(i * tq, tq)
        qt = (q_ref[pl.ds(q0, tq), :] * jnp.asarray(0.125, BF)).T
        qc = qc_ref[:, pl.ds(q0, tq)]
        qa = [jnp.concatenate([qt[64 * h:64 * h + 64], qc], axis=0) for h in range(nh)]

        def k_step(j, carry):
            k0 = pl.multiple_of(j * tk, tk)
            out = []
            for h in range(nh):
                m, l, acc = carry[h]
                s = dot(kaug[h, pl.ds(k0, tk), :], qa[h])
                mn = jnp.maximum(m, jnp.max(s, axis=0, keepdims=True))
                alpha = jnp.exp(m - mn)
                p = jnp.exp(s - mn)
                l = l * alpha + jnp.sum(p, axis=0, keepdims=True)
                acc = acc * alpha + dot(vt[64 * h:64 * h + 64, pl.ds(k0, tk)], p.astype(BF))
                out.append((mn, l, acc))
            return tuple(out)

        init = tuple((jnp.full((1, tq), NEG_FILL, F32), jnp.zeros((1, tq), F32), jnp.zeros((64, tq), F32)) for _ in range(nh))
        res = lax.fori_loop(lo_ref[i], hi_ref[i], k_step, init)
        outs = []
        for h in range(nh):
            m, l, acc = res[h]
            outs.append(acc / l)
            lse_ref[0, h:h + 1, pl.ds(q0, tq)] = m + jnp.log(l)
        o_ref[pl.ds(q0, tq), :] = jnp.concatenate(outs, axis=0).T.astype(BF)
        return 0

    lax.fori_loop(0, rows // tq, q_step, 0)


def attend_forward(qkv, lo, hi, keys, queries, heads, tq, tk, hp):
    rows = qkv.shape[0]
    pairs = heads // 2
    steps = pairs // hp
    col = lambda off: pl.BlockSpec((rows, 128 * hp), lambda h, *_: (0, off + h))
    return pl.pallas_call(
        functools.partial(fwd_kernel, tq=tq, tk=tk),
        out_shape=(jax.ShapeDtypeStruct((rows, heads * 64), BF), jax.ShapeDtypeStruct((steps, 2 * hp, rows), F32)),
        grid_spec=pltpu.PrefetchScalarGridSpec(
            num_scalar_prefetch=2,
            grid=(steps,),
            in_specs=[col(0), col(steps), col(2 * steps),
                      pl.BlockSpec((rows, 64), lambda h, *_: (0, 0)),
                      pl.BlockSpec((64, rows), lambda h, *_: (0, 0))],
            out_specs=[pl.BlockSpec((rows, 128 * hp), lambda h, *_: (0, h)),
                       pl.BlockSpec((1, 2 * hp, rows), lambda h, *_: (h, 0, 0))],
            scratch_shapes=[pltpu.VMEM((2 * hp, rows, 128), BF), pltpu.VMEM((128 * hp, rows), BF)],
        ),
        name="attend_forward",
    )(lo, hi, qkv, qkv, qkv, keys, queries)


def bwd_kernel(lo_ref, hi_ref, q_ref, k_ref, v_ref, g_ref, o_ref, lse_ref, kc_ref, qc_ref,
               dq_ref, dk_ref, dv_ref, kaug, kt, dk, dv, *, tq, tk):
    rows = q_ref.shape[0]
    nh = q_ref.shape[1] // 64
    kc = kc_ref[...]
    k = k_ref[...]
    for h in range(nh):
        kaug[h] = jnp.concatenate([k[:, 64 * h:64 * h + 64], kc], axis=1)
    kt[...] = k.T
    dk[...] = jnp.zeros_like(dk)
    dv[...] = jnp.zeros_like(dv)
    lane = lax.broadcasted_iota(jnp.int32, (tq, 128), 1)
    sub = lax.broadcasted_iota(jnp.int32, (128, tq), 0)

    def q_step(i, _):
        q0 = pl.multiple_of(i * tq, tq)
        q = q_ref[pl.ds(q0, tq), :] * jnp.asarray(0.125, BF)
        g = g_ref[pl.ds(q0, tq), :]
        qt = q.T
        gt = g.T
        prod = gt.astype(F32) * o_ref[pl.ds(q0, tq), :].T.astype(F32)
        qc = qc_ref[:, pl.ds(q0, tq)]
        zero = jnp.zeros((), BF)
        qa, ga, delta, lse = [], [], [], []
        for h in range(nh):
            qa.append(jnp.concatenate([qt[64 * h:64 * h + 64], qc], axis=0))
            gp = gt[128 * (h // 2):128 * (h // 2) + 128]
            ga.append(jnp.where(sub // 64 == h % 2, gp, zero))
            delta.append(jnp.sum(prod[64 * h:64 * h + 64], axis=0, keepdims=True))
            lse.append(lse_ref[0, h:h + 1, pl.ds(q0, tq)])
        qz = [jnp.concatenate([jnp.where(lane // 64 == h, q[:, 128 * w:128 * w + 128], zero) for h in range(2)], axis=0) for w in range(nh // 2)]
        gz = [jnp.concatenate([jnp.where(lane // 64 == h, g[:, 128 * w:128 * w + 128], zero) for h in range(2)], axis=0) for w in range(nh // 2)]

        def k_step(j, carry):
            k0 = pl.multiple_of(j * tk, tk)
            v = v_ref[pl.ds(k0, tk), :]
            ps, dss, dqs = [], [], []
            for h in range(nh):
                s = dot(kaug[h, pl.ds(k0, tk), :], qa[h])
                dp = dot(v[:, 128 * (h // 2):128 * (h // 2) + 128], ga[h])
                p = jnp.exp(s - lse[h])
                ds = (p * (dp - delta[h])).astype(BF)
                ps.append(p.astype(BF))
                dss.append(ds)
                dqs.append(carry[h] + dot(kt[64 * h:64 * h + 64, pl.ds(k0, tk)], ds))
            for w in range(nh // 2):
                dv[pl.ds(k0, tk), 128 * w:128 * w + 128] += dot(jnp.concatenate(ps[2 * w:2 * w + 2], axis=1), gz[w])
                dk[pl.ds(k0, tk), 128 * w:128 * w + 128] += dot(jnp.concatenate(dss[2 * w:2 * w + 2], axis=1), qz[w])
            return tuple(dqs)

        res = lax.fori_loop(lo_ref[i], hi_ref[i], k_step, tuple(jnp.zeros((64, tq), F32) for _ in range(nh)))
        dq_ref[pl.ds(q0, tq), :] = (jnp.concatenate(res, axis=0) * 0.125).T.astype(BF)
        return 0

    lax.fori_loop(0, rows // tq, q_step, 0)
    dk_ref[...] = dk[...].astype(BF)
    dv_ref[...] = dv[...].astype(BF)


def attend_backward(qkv, grad, mixed, lse, lo, hi, keys, queries, heads, tq, tk, hp):
    rows = qkv.shape[0]
    pairs = heads // 2
    steps = pairs // hp
    col = lambda off: pl.BlockSpec((rows, 128 * hp), lambda h, *_: (0, off + h))
    sd = jax.ShapeDtypeStruct((rows, heads * 64), BF)
    return pl.pallas_call(
        functools.partial(bwd_kernel, tq=tq, tk=tk),
        out_shape=(sd, sd, sd),
        grid_spec=pltpu.PrefetchScalarGridSpec(
            num_scalar_prefetch=2,
            grid=(steps,),
            in_specs=[col(0), col(steps), col(2 * steps), col(0), col(0),
                      pl.BlockSpec((1, 2 * hp, rows), lambda h, *_: (h, 0, 0)),
                      pl.BlockSpec((rows, 64), lambda h, *_: (0, 0)),
                      pl.BlockSpec((64, rows), lambda h, *_: (0, 0))],
            out_specs=[pl.BlockSpec((rows, 128 * hp), lambda h, *_: (0, h))] * 3,
            scratch_shapes=[pltpu.VMEM((2 * hp, rows, 128), BF), pltpu.VMEM((128 * hp, rows), BF),
                            pltpu.VMEM((rows, 128 * hp), F32), pltpu.VMEM((rows, 128 * hp), F32)],
        ),
        name="attend_backward",
    )(lo, hi, qkv, qkv, qkv, grad, mixed, lse, keys, queries)


def exact(a, b, dims):
    return lax.dot_general(a, b, dims, precision=HIGH, preferred_element_type=F32)


def contrast_kernel(
    place_ref, own_ref, other_ref, count_ref, loss_ref, grad_ref,
    anchors, positives, product, expos, square_a, row_sum, picks, parts, sums, *, slots, widths, block,
):
    me, tile = place_ref[0], place_ref[1]
    total = own_ref.shape[0]
    blocks = total // block
    full = (((1,), (0,)), ((), ()))
    col = lax.broadcasted_iota(jnp.int32, (block, total), 1)
    base = lax.broadcasted_iota(jnp.int32, (block, total), 0)
    shift = slots * tile.astype(F32)
    away = slots * (1 - tile).astype(F32)

    def masks(index):
        row = base + index * block
        real = (row % PAD_SLOTS < slots) & (col % PAD_SLOTS < slots)
        return row, real, jnp.where((row == col) & real, 1.0, 0.0)

    def start(index):
        return pl.multiple_of(index * block, block)

    def choose(index, across):
        at = pl.ds(start(index), block)
        row, real, eye = masks(index)
        numbers = own_ref[at, D:].astype(F32)
        local = (col % PAD_SLOTS).astype(F32)
        ok = (row // PAD_SLOTS == col // PAD_SLOTS) & real
        result = []
        for which, chosen in enumerate((anchors, positives)):
            number = numbers[:, which:which + 1]
            near_own = jnp.where(ok & (number == local + shift), 1.0, 0.0).astype(BF)
            near_other = jnp.where(ok & (number == local + away), 1.0, 0.0).astype(BF)
            chosen[at, :] = (dot(near_own, own_ref[:, :D]) + dot(near_other, other_ref[:, :D])).astype(BF)
            result.append(across[which] + jnp.sum(eye * number, axis=0, keepdims=True))
        return tuple(result)

    zero_row = jnp.zeros((1, total), F32)
    across = lax.fori_loop(0, blocks, choose, (zero_row, zero_row))
    srow = lax.broadcasted_iota(jnp.int32, (PAD_SLOTS, total), 0)
    scol = lax.broadcasted_iota(jnp.int32, (PAD_SLOTS, total), 1)
    mine = (scol // PAD_SLOTS == me) & (scol % PAD_SLOTS < slots) & (srow < slots)
    for which in range(2):
        picks[which] = jnp.where(mine & (across[which] == srow.astype(F32) + shift), 1.0, 0.0)
    product[...] = jnp.zeros_like(product)
    square_a[...] = jnp.zeros_like(square_a)
    square_b = zero_row
    good_col = jnp.where(scol[0:1] % PAD_SLOTS < slots, 1.0, 0.0)
    ones = jnp.ones((8, D), F32)
    losses = []
    begin = 0
    for place, end in enumerate(widths):
        cut = slice(begin, end)
        begin = end
        square_b = square_b + exact(ones[:, cut], positives[:, cut].astype(F32) ** 2, NT)[0:1]
        unit_b = lax.rsqrt(square_b + EPS_UNIT)

        def totals(index, carry):
            col_total, loss = carry
            at = pl.ds(start(index), block)
            row, real, eye = masks(index)
            front = anchors[at, cut]
            square_a[at, :] += jnp.sum(front.astype(F32) ** 2, axis=1, keepdims=True)
            product[at, :] += nt(front, positives[:, cut])
            sims = INV_TEMP * lax.rsqrt(square_a[at, :] + EPS_UNIT) * unit_b * product[at, :]
            expo = jnp.where(real, jnp.exp(sims - INV_TEMP), 0.0)
            expos[at, :] = expo
            good = row[:, 0:1] % PAD_SLOTS < slots
            row_total = jnp.where(good, jnp.sum(expo, axis=1, keepdims=True), 1.0)
            row_sum[at, :] = row_total
            row_log = jnp.where(good, INV_TEMP + jnp.log(row_total), 0.0)
            loss = loss + jnp.sum(row_log, axis=0, keepdims=True)
            diag = jnp.sum(jnp.sum(eye * sims, axis=0, keepdims=True), axis=1, keepdims=True)
            return col_total + jnp.sum(expo, axis=0, keepdims=True), loss - 2.0 * diag

        col_total, loss = lax.fori_loop(0, blocks, totals, (zero_row, jnp.zeros((1, 1), F32)))
        col_total = jnp.where(good_col > 0, col_total, 1.0)
        loss = loss + jnp.sum(good_col * (INV_TEMP + jnp.log(col_total)), axis=1, keepdims=True)
        losses.append(loss / (2.0 * slots * (total // PAD_SLOTS)))

        def grads(index, carry):
            pull_a, pull_b, part_b = carry
            at = pl.ds(start(index), block)
            row, real, eye = masks(index)
            unit_a = lax.rsqrt(square_a[at, :] + EPS_UNIT)
            scale = INV_TEMP * unit_a * unit_b
            expo = expos[at, :]
            share = 0.5 * (expo / row_sum[at, :] + expo / col_total) - eye
            toward = share * (scale * product[at, :])
            weight = scale * share
            pull = unit_a * unit_a * jnp.sum(toward, axis=1, keepdims=True)
            pull_a = pull_a + jnp.sum(eye * pull, axis=0, keepdims=True)
            pull_b = pull_b + jnp.sum(toward, axis=0, keepdims=True)
            parts[2 * place, :, at] = exact(picks[1], weight, NT)
            return pull_a, pull_b, part_b + exact(picks[0, :, at], weight, full)

        pull_a, pull_b, part_b = lax.fori_loop(
            0, blocks, grads, (zero_row, zero_row, jnp.zeros((PAD_SLOTS, total), F32)))
        parts[2 * place] = parts[2 * place] - picks[0] * pull_a
        parts[2 * place + 1] = part_b - picks[1] * (unit_b * unit_b * pull_b)
    spans = list(zip((0,) + tuple(widths[:-1]), widths))
    sums[...] = jnp.zeros_like(sums)
    counts = count_ref[:, 0:1]
    for place in range(len(widths) - 1, -1, -1):
        begin, end = spans[place]
        sums[0] += parts[2 * place]
        sums[1] += parts[2 * place + 1]
        grad = exact(sums[0], anchors[:, begin:end].astype(F32), full)
        grad += exact(sums[1], positives[:, begin:end].astype(F32), full)
        grad_ref[:, begin:end] = grad / counts
    lane = lax.broadcasted_iota(jnp.int32, (8, 128), 1)
    out = jnp.zeros((8, 128), F32)
    for place, loss in enumerate(losses):
        out = jnp.where(lane == len(widths) - 1 - place, loss, out)
    loss_ref[...] = out


def contrast(own, other, counts, me, tile, slots):
    widths = (D // 12, D // 6, D // 3, D * 2 // 3, D)
    total = own.shape[0]
    block = min(total, 256)
    whole = lambda shape: pl.BlockSpec(shape, lambda i, *_: (0,) * len(shape))
    return pl.pallas_call(
        functools.partial(contrast_kernel, slots=slots, widths=widths, block=block),
        out_shape=(jax.ShapeDtypeStruct((8, 128), F32), jax.ShapeDtypeStruct((PAD_SLOTS, D), F32)),
        grid_spec=pltpu.PrefetchScalarGridSpec(
            num_scalar_prefetch=1,
            grid=(1,),
            in_specs=[whole((total, own.shape[1])), whole((total, own.shape[1])), whole((PAD_SLOTS, 128))],
            out_specs=[whole((8, 128)), whole((PAD_SLOTS, D))],
            scratch_shapes=[
                pltpu.VMEM((total, D), BF), pltpu.VMEM((total, D), BF),
                pltpu.VMEM((total, total), F32), pltpu.VMEM((total, total), F32),
                pltpu.VMEM((total, 1), F32), pltpu.VMEM((total, 1), F32),
                pltpu.VMEM((2, PAD_SLOTS, total), F32), pltpu.VMEM((2 * len(widths), PAD_SLOTS, total), F32),
                pltpu.VMEM((2, PAD_SLOTS, total), F32)],
        ),
        name="contrast",
    )(jnp.stack([me, tile]).astype(jnp.int32), own, other, counts)


def layer_norm(value, gain, shift):
    center = value - jnp.mean(value, axis=-1, keepdims=True)
    spread = jnp.mean(center * center, axis=-1, keepdims=True)
    return center * lax.rsqrt(spread + EPS_NORM) * gain + shift


def shards(
    layer_input, segment_ids, pad_mask, pair_slots, result_cotangent,
    query_weight, key_weight, value_weight, output_weight,
    query_bias, value_bias, output_bias, first_gain, first_shift,
    inner_weight, inner_bias, outer_weight, outer_bias, second_gain, second_shift,
):
    rows = layer_input.shape[0]
    count, me = lax.axis_size("dp"), lax.axis_index("dp")
    tile = lax.axis_index("tile")
    slots = pair_slots.shape[0]
    own = query_weight.shape[0]
    fold = inner_weight.shape[1] // D
    valid = pad_mask == 1
    vectors = [query_bias, value_bias, output_bias, first_gain, first_shift, outer_bias, second_gain, second_shift]
    columns = jnp.concatenate(
        [v[:, None] for v in vectors] + [inner_bias.reshape(own, fold)]
        + [jnp.zeros((own, 128 - len(vectors) - fold), BF)], axis=1)
    early = gather_rows(jnp.concatenate([query_weight, key_weight, value_weight, columns], axis=1))
    inner_fold = inner_weight.reshape(own, D, fold).transpose(0, 2, 1).reshape(own, fold * D)
    late = lax.all_gather(
        jnp.concatenate([inner_fold, outer_weight.reshape(own, fold * D), output_weight], axis=1),
        ("dp", "tile"), axis=0, tiled=True)
    qkv_full = early[:, :3 * D]
    vec = early[:, 3 * D:].T.astype(F32)
    query_offset, value_offset, output_offset, gain_first, shift_first, outer_offset, gain_second, shift_second = (
        vec[i] for i in range(8))
    inner_offset = vec[8:8 + fold].reshape(fold * D)
    inner_full = late[:, :fold * D]
    outer_full = late[:, fold * D:2 * fold * D].reshape(D, fold, D).transpose(1, 0, 2).reshape(fold * D, D)
    output_full = late[:, 2 * fold * D:]

    keys, queries = mask_codes(segment_ids, valid, slots)
    offset = jnp.concatenate([query_offset, jnp.zeros((D,), F32), value_offset])
    qkv = (dot(layer_input, qkv_full) + offset).astype(BF)
    lo, hi = key_ranges(segment_ids, valid, *FWD_TILES[:2])
    mixed, log_totals = attend_forward(qkv, lo, hi, keys, queries, HEADS, *FWD_TILES)
    branch = dot(mixed, output_full) + output_offset
    hidden, first_back = jax.vjp(layer_norm, layer_input.astype(F32) + branch, gain_first, shift_first)
    hidden_low = hidden.astype(BF)
    inner = dot(hidden_low, inner_full) + inner_offset
    cdf = 0.5 * (1.0 + lax.erf(inner * (0.5 ** 0.5)))
    active = (inner * cdf).astype(BF)
    slope = (cdf + inner * jnp.exp(-0.5 * inner * inner) * 0.3989422804014327).astype(BF)
    outer = dot(active, outer_full) + outer_offset
    result, second_back = jax.vjp(layer_norm, hidden + outer, gain_second, shift_second)

    ids = jnp.arange(PAD_SLOTS, dtype=jnp.int32)
    member = ((segment_ids[None, :] == ids[:, None]) & valid[None, :]).astype(F32)
    counts = jnp.maximum(jnp.sum(member, axis=1, keepdims=True), 1.0)
    pooled = (jnp.dot(member, result, precision=HIGH) / counts).astype(BF)
    numbers = jnp.pad(pair_slots.astype(BF), ((0, PAD_SLOTS - slots), (0, 126)), constant_values=-1)
    packet = jnp.concatenate([pooled, numbers], axis=1)
    packets = lax.all_to_all(jnp.broadcast_to(packet[None], (count,) + packet.shape), "dp", 0, 0, tiled=True)
    packets = packets.reshape(count * PAD_SLOTS, packet.shape[1])
    loss_block, pooled_grad = contrast(
        packets, swap_tile(packets), jnp.broadcast_to(counts, (PAD_SLOTS, 128)), me, tile, slots)
    dim_losses = loss_block[0, :5]
    total_loss = jnp.sum(dim_losses)

    result_grad = result_cotangent.astype(F32) + lax.dot_general(
        member, pooled_grad, TN, precision=HIGH, preferred_element_type=F32)
    norm_grad, second_gain_grad, second_shift_grad = second_back(result_grad)
    outer_grad = norm_grad.astype(BF)
    outer_weight_grad = tn(active, outer_grad)
    outer_bias_grad = jnp.sum(outer_grad, axis=0, dtype=F32)
    inner_grad = (nt(outer_grad, outer_full) * slope.astype(F32)).astype(BF)
    inner_weight_grad = tn(hidden_low, inner_grad)
    inner_bias_grad = jnp.sum(inner_grad, axis=0, dtype=F32)
    feed = jnp.concatenate(
        [inner_weight_grad.astype(BF),
         outer_weight_grad.astype(BF).reshape(fold, D, D).transpose(1, 0, 2).reshape(D, fold * D)], axis=1)
    feed_shard = lax.psum_scatter(feed, ("dp", "tile"), scatter_dimension=0, tiled=True).astype(F32)
    hidden_grad = norm_grad + nt(inner_grad, inner_full)

    residual_grad, first_gain_grad, first_shift_grad = first_back(hidden_grad)
    branch_grad = residual_grad.astype(BF)
    output_weight_grad = tn(mixed, branch_grad)
    output_bias_grad = jnp.sum(branch_grad, axis=0, dtype=F32)
    mixed_grad = nt(branch_grad, output_full).astype(BF)
    lo, hi = key_ranges(segment_ids, valid, *BWD_TILES[:2])
    query_grad, key_grad, value_grad = attend_backward(
        qkv, mixed_grad, mixed, log_totals.reshape(-1, 2 * BWD_TILES[2], rows), lo, hi, keys, queries, HEADS, *BWD_TILES)
    vector_grads = jnp.stack(
        [jnp.sum(query_grad, axis=0, dtype=F32), jnp.sum(value_grad, axis=0, dtype=F32), output_bias_grad,
         first_gain_grad, first_shift_grad, outer_bias_grad, second_gain_grad, second_shift_grad]
        + [inner_bias_grad[i * D:(i + 1) * D] for i in range(fold)], axis=0)
    vector_grads = jnp.pad(vector_grads, ((0, 128 - vector_grads.shape[0]), (0, 0))).T
    attention_grads = jnp.concatenate(
        [tn(layer_input, query_grad).astype(BF), tn(layer_input, key_grad).astype(BF),
         tn(layer_input, value_grad).astype(BF), output_weight_grad.astype(BF), vector_grads.astype(BF)], axis=1)
    shard = scatter_rows(attention_grads)
    input_grad = (
        residual_grad + nt(query_grad, qkv_full[:, :D]) + nt(key_grad, qkv_full[:, D:2 * D])
        + nt(value_grad, qkv_full[:, 2 * D:]))
    small = shard[:, 4 * D:].T
    return (
        total_loss, dim_losses, result.astype(BF), input_grad,
        shard[:, :D], shard[:, D:2 * D], shard[:, 2 * D:3 * D], shard[:, 3 * D:4 * D],
        small[0], small[1], small[2], small[3], small[4],
        feed_shard[:, :fold * D].reshape(own, fold, D).transpose(0, 2, 1).reshape(own, fold * D),
        small[8:8 + fold].T.reshape(own * fold),
        feed_shard[:, fold * D:].reshape(own * fold, D),
        small[5], small[6], small[7],
    )


def solution(mesh):
    both = ("dp", "tile")
    wide, flat = P(both, None), P(both)
    return jax.shard_map(
        shards,
        mesh=mesh,
        in_specs=(wide, flat, flat, P("dp", None), wide, wide, wide, wide, wide)
        + (flat,) * 5 + (wide, flat, wide) + (flat,) * 3,
        out_specs=(P(), P(), wide, wide, wide, wide, wide, wide) + (flat,) * 5 + (wide, flat, wide) + (flat,) * 3,
        check_vma=False,
    )
```

time: 1750 us -> 516 us (0.29)
  waiting for transfers between devices: 543 us -> 67 us
  matrix products: 592 us -> 140 us
  blocking collectives: 209 us -> 32.4 us
  local copies, waits for them, and re-layouts: 232 us -> 71.6 us
  Pallas kernels: 0 us -> 114 us
  other arithmetic: 121 us -> 31.6 us
  starting transfers between devices: 10.2 us -> 33.6 us
    dot_general x165 -> x18, matrix products: 592 us -> 140 us  [the longest x6 49.6 us: nt(): return lax.dot_general(a, b, NT, preferred_element_type=F32)]
    all_gather x12 -> x1, waiting for transfers between devices: 202 us -> 0.01 us  [shards(): lax.all_gather(jnp.concatenate([inner_fold, outer_weight.reshape(own, fol...]
    unnamed x26 -> x2, waiting for transfers between devices: 199 us -> 0.03 us
    reduce_scatter x3 -> x1, waiting for transfers between devices: 142 us -> 0.01 us  [shards(): lax.psum_scatter(feed, ('dp', 'tile'), scatter_dimension=0, tiled=True)]
    pallas_call x0 -> x4, Pallas kernels: none -> 114 us  [the longest x1 59.2 us: attend_backward(): pl.pallas_call(functools.partial(bwd_kernel, tq=tq, tk=tk), out_shape=(sd...]
    unnamed x3 -> x0, blocking collectives: 87.7 us -> none
    psum x3 -> x0, blocking collectives: 79.1 us -> none  [the longest x1 40.1 us: shards(): dim_losses = lax.psum(local_terms, ('dp', 'tile')) / (slots * dp_count)]
    ppermute x0 -> x18, waiting for transfers between devices: none -> 67 us  [the longest x12 66.9 us: send_to(): lax.ppermute(value, 'dp', [(i, peer(i, stride, radix, step)) for i in ran...]
  transfers between devices with their start and end apart: 23 -> 20, of which waited for: 8 -> 11; matrix products, arithmetic and copies ran while one was open for 49% -> 21% of each run, Pallas kernels for 0% -> 21%
where the time goes in v1:
time: 516 us; the launch traced here: 506 us
  matrix products  140 us (27%)
  Pallas kernels  114 us (22%)
  local copies, waits for them, and re-layouts  71.6 us (14%)
  waiting for transfers between devices  67 us (13%)
  starting transfers between devices  33.6 us (7%)
  blocking collectives  32.4 us (6%)
  other arithmetic  31.6 us (6%)
  between operations  15.2 us (3%)
    ppermute x12, waiting for transfers between devices, send_to(): lax.ppermute(value, 'dp', [(i, peer(i, stride, radix, step)) for i in ran...  66.9 us
    pallas_call x1, Pallas kernels, attend_backward(): pl.pallas_call(functools.partial(bwd_kernel, tq=tq, tk=tk), out_shape=(sd...  59.2 us
    dot_general x6, matrix products, nt(): return lax.dot_general(a, b, NT, preferred_element_type=F32)  49.6 us
    dot_general x4, matrix products, dot(): return jnp.dot(a, b, preferred_element_type=F32)  45.3 us
    pallas_call x1, Pallas kernels, attend_forward(): pl.pallas_call(functools.partial(fwd_kernel, tq=tq, tk=tk), out_shape=(ja...  41.3 us
    dot_general x6, matrix products, tn(): return lax.dot_general(a, b, TN, preferred_element_type=F32)  36.5 us
    all_to_all x1, blocking collectives, shards(): lax.all_to_all(jnp.broadcast_to(packet[None], (count,) + packet.shape), '...  32.4 us
    ppermute x12, starting transfers between devices, send_to(): lax.ppermute(value, 'dp', [(i, peer(i, stride, radix, step)) for i in ran...  24 us
  transfers between devices with their start and end apart: 20, of which 11 were waited for; matrix products, arithmetic and copies ran while one was open for 21% of the time, Pallas kernels for 21%

profile of v1, /device:TPU:0, one launch (start us, length us, event | category | flops | bytes accessed | tf_op | source)
XLA Modules:
  0.0 506.0 jit_solution(17416472939880085822)
XLA Ops:
  7.3 1.2 reshape.196
  8.4 1.3 copy.153
  10.3 1.5 pad_maximum_fusion.2
  19.5 5.1 %collective-permute-start.2 = (bf16[1,24,2432]{2,1,0:T(8,128)(2,1)S(1)}, bf16[1,24,2432]{2,1,0:T(8,128)(2,1)S(1)}, u32[]{:S(2)}, u32[]{:S(2)}) collective-permute-start(bf16[1,24,2432]{2,1,0:T(8,128)(2,1)S(1)} %bitcast.157), channel_id=1, source_target_pairs={{0,24},{2,26},{4,28},{6,30},{8,16},{10,18},{12,20},{14,22},{16,8},... | collective-permute-start | bytes 350216 | tf_op jit(solution)/shard_map/ppermute | solution.py:61
  29.6 10.7 %collective-permute-done.1 = bf16[1,24,2432]{2,1,0:T(8,128)(2,1)S(1)} collective-permute-done((bf16[1,24,2432]{2,1,0:T(8,128)(2,1)S(1)}, bf16[1,24,2432]{2,1,0:T(8,128)(2,1)S(1)}, u32[]{:S(2)}, u32[]{:S(2)}) %collective-permute-start.1) | collective-permute-done | bytes 116768 | tf_op jit(solution)/shard_map/ppermute | solution.py:61
  40.4 2.3 collective-permute-start.5
  44.8 15.2 %collective-permute-done.5.refs_3_ = bf16[4,24,2432]{2,1,0:T(8,128)(2,1)} collective-permute-done((bf16[4,24,2432]{2,1,0:T(8,128)(2,1)S(1)}, bf16[4,24,2432]{2,1,0:T(8,128)(2,1)}, u32[]{:S(2)}, u32[]{:S(2)}) %collective-permute-start.5) | collective-permute-done | bytes 466976 | tf_op jit(solution)/shard_map/ppermute | solution.py:61
  59.9 7.1 %collective-permute-done.4.refs_2_ = bf16[4,24,2432]{2,1,0:T(8,128)(2,1)} collective-permute-done((bf16[4,24,2432]{2,1,0:T(8,128)(2,1)S(1)}, bf16[4,24,2432]{2,1,0:T(8,128)(2,1)}, u32[]{:S(2)}, u32[]{:S(2)}) %collective-permute-start.4) | collective-permute-done | bytes 466976 | tf_op jit(solution)/shard_map/ppermute | solution.py:61
  67.1 4.8 collective-permute-done.3.refs_1_
  72.0 2.5 copy.142
  76.2 4.9 place_rows.1
  82.5 9.6 %fusion.5.q_ref.k_ref.v_ref = bf16[1536,2304]{1,0:T(8,128)(2,1)} fusion(bf16[1536,768]{1,0:T(8,128)(2,1)S(1)} %copy-done.9, f32[2304]{0:T(1024)S(1)} %pad_maximum_fusion.3, bf16[768,2432]{1,0:T(8,128)(2,1)} %bitcast.142), kind=kOutput, calls=%fused_computation.10 | convolution fusion | flops 5442895872 | bytes 12985344 | tf_op jit(solution)/shard_map/dot_general | solution.py:28
  92.1 41.3 %attend_forward.1 = (bf16[1536,768]{1,0:T(8,128)(2,1)}, f32[3,4,1536]{2,1,0:T(4,128)}) custom-call(s32[3]{0:T(128)} %get-tuple-element.194.lo_ref, s32[3]{0:T(128)} %get-tuple-element.193.hi_ref, bf16[1536,2304]{1,0:T(8,128)(2,1)} %fusion.5.q_ref.k_ref.v_ref, bf16[1536,2304]{1,0:T(8,128)(2,1)} %fusion.5.q_ref.k_ref.v_ref, ...), custom_call_target="tpu_custom_call" | custom-call | tf_op jit(solution)/shard_map/attend_forward/pallas_call | solution.py:210
  133.5 4.8 slice.181
  138.3 6.7 %copy.155 = bf16[768,3072]{0,1:T(8,128)(2,1)} copy(bf16[768,3072]{1,0:T(8,128)(2,1)} %slice.181) | data formatting | bytes 9437184 | tf_op jit(solution)/shard_map/slice | solution.py:488
  145.0 6.8 %copy.156 = bf16[4,768,768]{2,1,0:T(8,128)(2,1)} copy(bf16[4,768,768]{1,2,0:T(8,128)(2,1)} %bitcast.134) | data formatting | bytes 9437184 | tf_op jit(solution)/shard_map/transpose | solution.py:488
  151.7 4.3 fusion.66
  156.6 18.6 %multiply_convert_fusion.1 = (bf16[1536,3072]{1,0:T(8,128)(2,1)}, f32[1536,3072]{1,0:T(8,128)}) fusion(f32[3072]{0:T(1024)S(1)} %add.449, bf16[768,6912]{1,0:T(8,128)(2,1)} %all-gather.2.cloned.1.call-done, f32[1536,768]{0,1:T(8,128)S(1)} %get-tuple-element.184, f32[768]{0:T(1024)S(1)} %get-tuple-element.137, f32[768]{0:T(1024)S(1)} %get-tuple-element.138, ...), kind=kOutput, calls=%fused_computation.7 | convolution fusion | flops 7281967104 | bytes 37779456 | tf_op jit(solution)/shard_map/dot_general | solution.py:28
  175.2 12.8 %fusion.67 = (f32[1536]{0:T(1024)S(1)}, f32[1536,768]{0,1:T(8,128)S(1)}) fusion(f32[768]{0:T(1024)S(1)} %get-tuple-element.136, bf16[1536,3072]{1,0:T(8,128)(2,1)} %get-tuple-element.185, bf16[3072,768]{1,0:T(8,128)(2,1)} %bitcast.147, f32[768]{0:T(1024)S(1)} %get-tuple-element.137, f32[768]{0:T(1024)S(1)} %get-tuple-element.138, f32[1536]{0:T(1024)S(1)} %fusion.55, ...), kind=kOutput, calls=%fused_computation.155 | convolution fusion | flops 7256013312 | bytes 23620608 | tf_op jit(solution)/shard_map/dot_general | solution.py:28
  188.6 2.9 fusion.41
  191.5 32.4 %all_to_all.5 = bf16[16,16,896]{2,1,0:T(8,128)(2,1)S(1)} all-to-all(bf16[16,16,896]{2,1,0:T(8,128)(2,1)S(1)} %broadcast_in_dim.102), channel_id=1, replica_groups=mesh['dp'=16,'tile'=2] {'dp'}, dimensions={0} | all-to-all | bytes 917504 | tf_op jit(solution)/shard_map/all_to_all | solution.py:512
  223.9 3.0 copy.158
  229.0 9.1 %contrast.1 = (f32[8,128]{1,0:T(8,128)}, f32[16,768]{1,0:T(8,128)}) custom-call(s32[2]{0:T(128)} %pad_add_fusion.place_ref, bf16[256,896]{1,0:T(8,128)(2,1)} %bitcast.154, bf16[256,896]{1,0:T(8,128)(2,1)} %copy-done.13, f32[16,128]{1,0:T(8,128)} %broadcast_in_dim.103.count_ref), custom_call_target="tpu_custom_call" | custom-call | tf_op jit(solution)/shard_map/contrast/pallas_call | solution.py:435
  238.1 5.8 %multiply_reduce_fusion = (bf16[768]{0:T(1024)(128)(2,1)S(1)}, f32[1536]{0:T(1024)S(1)}, bf16[768]{0:T(1024)(128)(2,1)S(1)}, f32[1536,768]{0,1:T(8,128)S(1)}) fusion(f32[1536,768]{0,1:T(8,128)} %copy-done, f32[1536]{0:T(1024)S(1)} %fusion.56, f32[1536]{0:T(1024)S(1)} %broadcast_multiply_fusion, f32[768]{0:T(1024)S(1)} %get-tuple-element.134, ...), kind=kOutput, calls=%fused_computation.18 | convolution fusion | flops 238334976 | bytes 11877888 | tf_op jit(solution)/shard_map/dot_general | solution.py:519
  243.9 3.3 fusion.62
  247.7 11.1 %convolution_convert_fusion = bf16[3072,768]{1,0:T(8,128)(2,1)S(1)} fusion(bf16[1536,3072]{1,0:T(8,128)(2,1)} %get-tuple-element.185, bf16[1536,768]{0,1:T(8,128)(2,1)S(1)} %get-tuple-element.155), kind=kOutput, calls=%fused_computation.14 | convolution fusion | flops 7250116608 | bytes 16515072 | tf_op jit(solution)/shard_map/dot_general | solution.py:36
  258.8 16.9 %fusion.68 = (bf16[3072]{0:T(1024)(128)(2,1)S(1)}, bf16[1536,3072]{1,0:T(8,128)(2,1)}) fusion(f32[1536,3072]{1,0:T(8,128)} %get-tuple-element.186, f32[3072]{0:T(1024)S(1)} %add.449, bf16[1536,768]{0,1:T(8,128)(2,1)S(1)} %get-tuple-element.155, bf16[3072,768]{1,0:T(8,128)(2,1)S(1)} %bitcast.150), kind=kOutput, calls=%fused_computation.156 | convolution fusion | flops 7313814528 | bytes 35407872 | tf_op jit(solution)/shard_map/dot_general | solution.py:32
  275.7 3.6 copy.165
  279.3 1.0 copy.179
  280.4 10.4 %convolution_convert_fusion.1 = bf16[768,3072]{1,0:T(8,128)(2,1)S(1)} fusion(bf16[1536,3072]{1,0:T(8,128)(2,1)} %get-tuple-element.192, f32[1536,768]{0,1:T(8,128)S(1)} %bitcast.137, f32[768]{0:T(1024)S(1)} %get-tuple-element.137, f32[768]{0:T(1024)S(1)} %get-tuple-element.138, f32[1536]{0:T(1024)S(1)} %fusion.55, f32[1536]{0:T(1024)S(1)} %broadcast_multiply_fusion.1), kind=kOutput, calls=%fused_computation.15 | convolution fusion | flops 7256014848 | bytes 18892800 | tf_op jit(solution)/shard_map/dot_general | solution.py:36
  290.8 14.2 %multiply_reduce_fusion.1 = (bf16[768]{0:T(1024)(128)(2,1)S(1)}, f32[1536]{0:T(1024)S(1)}, bf16[768]{0:T(1024)(128)(2,1)S(1)}, f32[1536,768]{0,1:T(8,128)}) fusion(f32[1536,768]{0,1:T(8,128)S(1)} %bitcast.137, f32[1536]{0:T(1024)S(1)} %fusion.55, f32[1536]{0:T(1024)S(1)} %broadcast_multiply_fusion.1, f32[768]{0:T(1024)S(1)} %get-tuple-element.138, ...), kind=kOutput, calls=%fused_computation.19 | convolution fusion | flops 7259550720 | bytes 28342272 | tf_op jit(solution)/shard_map/dot_general | solution.py:32
  305.1 3.9 pad_maximum_fusion
  309.0 5.0 fusion.61
  314.7 5.7 %convolution_convert_fusion.2.g_ref = bf16[1536,768]{1,0:T(8,128)(2,1)} fusion(bf16[1536,768]{0,1:T(8,128)(2,1)S(1)} %get-tuple-element.157, bf16[768,6912]{1,0:T(8,128)(2,1)} %all-gather.2.cloned.1.call-done), kind=kOutput, calls=%fused_computation.41 | convolution fusion | flops 1813118976 | bytes 5898240 | tf_op jit(solution)/shard_map/dot_general | solution.py:32
  320.4 59.2 %attend_backward.1 = (bf16[1536,768]{1,0:T(8,128)(2,1)}, bf16[1536,768]{1,0:T(8,128)(2,1)}, bf16[1536,768]{1,0:T(8,128)(2,1)}) custom-call(s32[3]{0:T(128)} %get-tuple-element.194.lo_ref, s32[3]{0:T(128)} %get-tuple-element.193.hi_ref, bf16[1536,2304]{1,0:T(8,128)(2,1)} %fusion.5.q_ref.k_ref.v_ref, bf16[1536,2304]{1,0:T(8,128)(2,1)} %fusion.5.q_ref.k_ref.v_ref, ...), custom_call_target="tpu_custom_call" | custom-call | tf_op jit(solution)/shard_map/attend_backward/pallas_call | solution.py:292
  379.6 2.1 reduce.1
  381.7 2.1 reduce.2
  383.9 5.8 %fusion.24 = bf16[768,3200]{0,1:T(8,128)(2,1)} fusion(bf16[1536,768]{1,0:T(8,128)(2,1)} %get-tuple-element.30, bf16[1536,768]{1,0:T(8,128)(2,1)} %param.20), kind=kOutput, calls=%fused_computation.54 | convolution fusion | flops 1812529152 | bytes 5898240 | tf_op jit(solution)/shard_map/dot_general | solution.py:36
  389.7 3.1 fusion.26
  392.9 3.1 fusion.28
  396.0 3.0 fusion.22
  399.7 7.6 %copy.164 = bf16[768,3200]{1,0:T(8,128)(2,1)} copy(bf16[768,3200]{0,1:T(8,128)(2,1)} %bitcast_dynamic-update-slice_fusion) | data formatting | bytes 9830400 | tf_op jit(solution)/shard_map/concatenate | solution.py:547
  407.3 3.4 dynamic-slice_bitcast_fusion
  410.7 9.5 %collective-permute-start.11 = (bf16[16,24,3200]{2,1,0:T(8,128)(2,1)}, bf16[16,24,3200]{2,1,0:T(8,128)(2,1)}, u32[]{:S(2)}, u32[]{:S(2)}) collective-permute-start(bf16[16,24,3200]{2,1,0:T(8,128)(2,1)} %dynamic-slice_bitcast_fusion), channel_id=1, source_target_pairs={{0,1},{1,0},{2,3},{3,2},{4,5},{5,4},{6,7},{7,6},{8,9},{9,8},{10,11... | collective-permute-start | bytes 7372808 | tf_op jit(solution)/shard_map/ppermute | solution.py:65
  420.2 2.7 copy.167
  422.9 4.2 fusion.36
  427.1 4.3 fusion.38
  431.4 2.5 fusion.6
  433.9 1.3 dynamic-slice_bitcast_fusion.3
  435.2 9.4 %collective-permute-start.12 = (bf16[4,24,3200]{2,1,0:T(8,128)(2,1)}, bf16[4,24,3200]{2,1,0:T(8,128)(2,1)S(1)}, u32[]{:S(2)}, u32[]{:S(2)}) collective-permute-start(bf16[4,24,3200]{2,1,0:T(8,128)(2,1)} %get-tuple-element.165), channel_id=1, source_target_pairs={{0,2},{2,0},{4,6},{6,4},{8,10},{10,8},{12,14},{14,12},{16,18},{18,... | collective-permute-start | bytes 1843208 | tf_op jit(solution)/shard_map/ppermute | solution.py:61
  444.6 1.8 collective-permute-start.14
  446.4 4.3 add_add_fusion.2
  450.7 6.0 %copy.168 = f32[1536,768]{1,0:T(8,128)} copy(f32[1536,768]{0,1:T(8,128)} %add_add_fusion.2) | data formatting | bytes 9437184
  456.8 2.7 collective-permute-done.12
  459.4 14.3 %collective-permute-done.14 = bf16[4,24,3200]{2,1,0:T(8,128)(2,1)} collective-permute-done((bf16[4,24,3200]{2,1,0:T(8,128)(2,1)}, bf16[4,24,3200]{2,1,0:T(8,128)(2,1)}, u32[]{:S(2)}, u32[]{:S(2)}) %collective-permute-start.14) | collective-permute-done | bytes 614432 | tf_op jit(solution)/shard_map/ppermute | solution.py:61
  473.7 1.4 collective-permute-done.13
  475.1 1.6 fusion.31
  476.7 1.4 collective-permute-start.15
  479.0 1.2 collective-permute-start.16
  480.3 1.8 slice_bitcast_fusion.2
  482.1 3.1 collective-permute-done.15
  485.2 1.7 collective-permute-done.17
  486.9 5.7 %collective-permute-done.16 = bf16[1,24,3200]{2,1,0:T(8,128)(2,1)S(1)} collective-permute-done((bf16[1,24,3200]{2,1,0:T(8,128)(2,1)S(1)}, bf16[1,24,3200]{2,1,0:T(8,128)(2,1)S(1)}, u32[]{:S(2)}, u32[]{:S(2)}) %collective-permute-start.16) | collective-permute-done | bytes 153632 | tf_op jit(solution)/shard_map/ppermute | solution.py:61
  497.5 1.2 copy.169
  (161 shorter events, 29.6 us)
Async XLA Ops:
  7.2 36.8 %copy-start.14 = (s32[1536]{0:T(1024)S(1)}, s32[1536]{0:T(1024)}, u32[]{:S(2)}) copy-start(s32[1536]{0:T(1024)} %param.21) | copy-start | bytes 18436
  7.2 64.7 %copy-start.16 = (s32[12,2]{0,1:T(2,128)S(1)}, s32[12,2]{0,1:T(2,128)}, u32[]{:S(2)}) copy-start(s32[12,2]{0,1:T(2,128)} %param.23) | copy-start | bytes 292
  7.2 64.8 %copy-start.9 = (bf16[1536,768]{1,0:T(8,128)(2,1)S(1)}, bf16[1536,768]{1,0:T(8,128)(2,1)}, u32[]{:S(2)}) copy-start(bf16[1536,768]{1,0:T(8,128)(2,1)} %param.20) | copy-start | bytes 7077892
  7.2 126.2 %all-gather.2.cloned.1.call-start = ((), (), s32[]{:S(2)}) async-start(), calls=%async_computation.2 | async-start | bytes 10948608 | tf_op jit(solution)/shard_map/all_gather | solution.py:479
  11.8 483.0 %reduce-scatter.2.cloned.1.call-start = ((), (), s32[]{:S(2)}) async-start(), calls=%async_computation.3 | async-start | bytes 9732096 | tf_op jit(solution)/shard_map/reduce_scatter | solution.py:531
  19.5 10.1 %collective-permute-start.2 = (bf16[1,24,2432]{2,1,0:T(8,128)(2,1)S(1)}, bf16[1,24,2432]{2,1,0:T(8,128)(2,1)S(1)}, u32[]{:S(2)}, u32[]{:S(2)}) collective-permute-start(bf16[1,24,2432]{2,1,0:T(8,128)(2,1)S(1)} %bitcast.157), channel_id=1, source_target_pairs={{0,24},{2,26},{4,28},{6,30},{8,16},{10,18},{12,20},{14,22},{16,8},... | collective-permute-start | bytes 350216 | tf_op jit(solution)/shard_map/ppermute | solution.py:61
  24.6 15.7 %collective-permute-start.1 = (bf16[1,24,2432]{2,1,0:T(8,128)(2,1)S(1)}, bf16[1,24,2432]{2,1,0:T(8,128)(2,1)S(1)}, u32[]{:S(2)}, u32[]{:S(2)}) collective-permute-start(bf16[1,24,2432]{2,1,0:T(8,128)(2,1)S(1)} %bitcast.158), channel_id=1, source_target_pairs={{0,16},{2,18},{4,20},{6,22},{8,24},{10,26},{12,28},{14,30},{16,0},... | collective-permute-start | bytes 350216 | tf_op jit(solution)/shard_map/ppermute | solution.py:61
  24.6 15.7 %collective-permute-start = (bf16[1,24,2432]{2,1,0:T(8,128)(2,1)S(1)}, bf16[1,24,2432]{2,1,0:T(8,128)(2,1)S(1)}, u32[]{:S(2)}, u32[]{:S(2)}) collective-permute-start(bf16[1,24,2432]{2,1,0:T(8,128)(2,1)S(1)} %bitcast.159), channel_id=1, source_target_pairs={{0,8},{2,10},{4,12},{6,14},{8,0},{10,2},{12,4},{14,6},{16,24},{18,... | collective-permute-start | bytes 350216 | tf_op jit(solution)/shard_map/ppermute | solution.py:61
  40.4 35.9 %copy-start.11 = (bf16[4,24,2432]{2,1,0:T(8,128)(2,1)}, bf16[4,24,2432]{2,1,0:T(8,128)(2,1)S(1)}, u32[]{:S(2)}) copy-start(bf16[4,24,2432]{2,1,0:T(8,128)(2,1)S(1)} %pad_maximum_fusion.1.refs_0_) | copy-start | bytes 1400836
  40.4 19.5 %collective-permute-start.5 = (bf16[4,24,2432]{2,1,0:T(8,128)(2,1)S(1)}, bf16[4,24,2432]{2,1,0:T(8,128)(2,1)}, u32[]{:S(2)}, u32[]{:S(2)}) collective-permute-start(bf16[4,24,2432]{2,1,0:T(8,128)(2,1)S(1)} %pad_maximum_fusion.1.refs_0_), channel_id=1, source_target_pairs={{0,6},{2,4},{4,2},{6,0},{8,14},{10,12},{12,10},{14,8},{16,22},{18,... | collective-permute-start | bytes 1400840 | tf_op jit(solution)/shard_map/ppermute | solution.py:61
  42.7 24.3 %collective-permute-start.4 = (bf16[4,24,2432]{2,1,0:T(8,128)(2,1)S(1)}, bf16[4,24,2432]{2,1,0:T(8,128)(2,1)}, u32[]{:S(2)}, u32[]{:S(2)}) collective-permute-start(bf16[4,24,2432]{2,1,0:T(8,128)(2,1)S(1)} %pad_maximum_fusion.1.refs_0_), channel_id=1, source_target_pairs={{0,4},{2,6},{4,0},{6,2},{8,12},{10,14},{12,8},{14,10},{16,20},{18,... | collective-permute-start | bytes 1400840 | tf_op jit(solution)/shard_map/ppermute | solution.py:61
  43.0 28.9 %collective-permute-start.3 = (bf16[4,24,2432]{2,1,0:T(8,128)(2,1)S(1)}, bf16[4,24,2432]{2,1,0:T(8,128)(2,1)}, u32[]{:S(2)}, u32[]{:S(2)}) collective-permute-start(bf16[4,24,2432]{2,1,0:T(8,128)(2,1)S(1)} %pad_maximum_fusion.1.refs_0_), channel_id=1, source_target_pairs={{0,2},{2,0},{4,6},{6,4},{8,10},{10,8},{12,14},{14,12},{16,18},{18,... | collective-permute-start | bytes 1400840 | tf_op jit(solution)/shard_map/ppermute | solution.py:61
  44.8 31.5 %collective-permute-start.6 = (bf16[4,24,2432]{2,1,0:T(8,128)(2,1)S(1)}, bf16[4,24,2432]{2,1,0:T(8,128)(2,1)}, u32[]{:S(2)}, u32[]{:S(2)}) collective-permute-start(bf16[4,24,2432]{2,1,0:T(8,128)(2,1)S(1)} %pad_maximum_fusion.1.refs_0_), channel_id=1, source_target_pairs={{0,1},{1,0},{2,3},{3,2},{4,5},{5,4},{6,7},{7,6},{8,9},{9,8},{10,11... | collective-permute-start | bytes 1400840 | tf_op jit(solution)/shard_map/ppermute | solution.py:65
  59.9 16.3 %collective-permute-start.9 = (bf16[4,24,2432]{2,1,0:T(8,128)(2,1)}, bf16[4,24,2432]{2,1,0:T(8,128)(2,1)}, u32[]{:S(2)}, u32[]{:S(2)}) collective-permute-start(bf16[4,24,2432]{2,1,0:T(8,128)(2,1)} %collective-permute-done.5.refs_3_), channel_id=1, source_target_pairs={{0,1},{1,0},{2,3},{3,2},{4,5},{5,4},{6,7},{7,6},{8,9},{9,8},{10,11... | collective-permute-start | bytes 1400840 | tf_op jit(solution)/shard_map/ppermute | solution.py:65
  67.0 9.2 %collective-permute-start.8 = (bf16[4,24,2432]{2,1,0:T(8,128)(2,1)}, bf16[4,24,2432]{2,1,0:T(8,128)(2,1)}, u32[]{:S(2)}, u32[]{:S(2)}) collective-permute-start(bf16[4,24,2432]{2,1,0:T(8,128)(2,1)} %collective-permute-done.4.refs_2_), channel_id=1, source_target_pairs={{0,1},{1,0},{2,3},{3,2},{4,5},{5,4},{6,7},{7,6},{8,9},{9,8},{10,11... | collective-permute-start | bytes 1400840 | tf_op jit(solution)/shard_map/ppermute | solution.py:65
  71.9 4.3 collective-permute-start.7
  145.0 6.8 %copy-start.7 = (bf16[1536,768]{1,0:T(8,128)(2,1)S(1)}, bf16[1536,768]{1,0:T(8,128)(2,1)}, u32[]{:S(2)}) copy-start(bf16[1536,768]{1,0:T(8,128)(2,1)} %get-tuple-element.26.o_ref) | copy-start | bytes 7077892
  156.0 19.1 %copy-start.2 = (f32[1536,768]{0,1:T(8,128)}, f32[1536,768]{0,1:T(8,128)S(1)}, u32[]{:S(2)}) copy-start(f32[1536,768]{0,1:T(8,128)S(1)} %get-tuple-element.184) | copy-start | bytes 14155780
  188.0 3.5 copy-start
  223.9 5.1 copy-start.12
  223.9 3.6 collective-permute-start.10
  227.5 0.8 copy-start.13
  229.0 14.9 %slice-start = ((s8[4718592]{0:T(1024)(128)(4,1)}), s8[524288]{0:T(1024)(128)(4,1)S(1)}, s32[]{:S(2)}) async-start(s8[4718592]{0:T(1024)(128)(4,1)} %bitcast.126), calls=%async_computation.4 | async-start | bytes 1048576
  238.1 5.8 %slice-start.1 = ((s8[4718592]{0:T(1024)(128)(4,1)}), s8[4194304]{0:T(1024)(128)(4,1)S(1)}, s32[]{:S(2)}) async-start(s8[4718592]{0:T(1024)(128)(4,1)} %bitcast.126), calls=%async_computation.5 | async-start | bytes 8388608
  247.2 11.6 %slice-start.8 = ((s8[4718592]{0:T(1024)(128)(4,1)}), s8[4194304]{0:T(1024)(128)(4,1)S(1)}, s32[]{:S(2)}) async-start(s8[4718592]{0:T(1024)(128)(4,1)} %bitcast.148), calls=%async_computation.12 | async-start | bytes 8388608
  247.7 11.1 %slice-start.9 = ((s8[4718592]{0:T(1024)(128)(4,1)}), s8[524288]{0:T(1024)(128)(4,1)S(1)}, s32[]{:S(2)}) async-start(s8[4718592]{0:T(1024)(128)(4,1)} %bitcast.148), calls=%async_computation.13 | async-start | bytes 1048576
  275.7 4.7 slice-start.6
  279.3 1.1 slice-start.7
  314.0 6.3 %copy-start.1 = (f32[1536,768]{0,1:T(8,128)}, f32[1536,768]{0,1:T(8,128)S(1)}, u32[]{:S(2)}) copy-start(f32[1536,768]{0,1:T(8,128)S(1)} %get-tuple-element.159) | copy-start | bytes 14155780
  383.9 5.8 %copy-start.10 = (bf16[1536,768]{1,0:T(8,128)(2,1)S(1)}, bf16[1536,768]{1,0:T(8,128)(2,1)}, u32[]{:S(2)}) copy-start(bf16[1536,768]{1,0:T(8,128)(2,1)} %param.20) | copy-start | bytes 7077892
  383.9 5.8 %copy-start.15 = (bf16[1536,768]{1,0:T(8,128)(2,1)S(1)}, bf16[1536,768]{1,0:T(8,128)(2,1)}, u32[]{:S(2)}) copy-start(bf16[1536,768]{1,0:T(8,128)(2,1)} %get-tuple-element.31) | copy-start | bytes 7077892
  389.7 3.2 copy-start.4
  392.9 3.1 copy-start.8
  407.3 12.9 %copy-start.3 = (bf16[1536,768]{0,1:T(8,128)(2,1)S(1)}, bf16[1536,768]{0,1:T(8,128)(2,1)}, u32[]{:S(2)}) copy-start(bf16[1536,768]{0,1:T(8,128)(2,1)} %get-tuple-element.164) | copy-start | bytes 7077892
  410.7 20.7 %collective-permute-start.11 = (bf16[16,24,3200]{2,1,0:T(8,128)(2,1)}, bf16[16,24,3200]{2,1,0:T(8,128)(2,1)}, u32[]{:S(2)}, u32[]{:S(2)}) collective-permute-start(bf16[16,24,3200]{2,1,0:T(8,128)(2,1)} %dynamic-slice_bitcast_fusion), channel_id=1, source_target_pairs={{0,1},{1,0},{2,3},{3,2},{4,5},{5,4},{6,7},{7,6},{8,9},{9,8},{10,11... | collective-permute-start | bytes 7372808 | tf_op jit(solution)/shard_map/ppermute | solution.py:65
  422.9 4.2 copy-start.6
  422.9 8.5 %slice-start.4 = ((s8[4915200]{0:T(1024)(128)(4,1)}), s8[4194304]{0:T(1024)(128)(4,1)S(1)}, s32[]{:S(2)}) async-start(s8[4915200]{0:T(1024)(128)(4,1)} %bitcast.131), calls=%async_computation.8 | async-start | bytes 8388608
  422.9 23.5 %slice-start.2 = ((s8[4718592]{0:T(1024)(128)(4,1)}), s8[4194304]{0:T(1024)(128)(4,1)S(1)}, s32[]{:S(2)}) async-start(s8[4718592]{0:T(1024)(128)(4,1)} %bitcast.128), calls=%async_computation.6 | async-start | bytes 8388608
  427.1 4.3 slice-start.5
  427.1 19.3 %slice-start.3 = ((s8[4718592]{0:T(1024)(128)(4,1)}), s8[524288]{0:T(1024)(128)(4,1)S(1)}, s32[]{:S(2)}) async-start(s8[4718592]{0:T(1024)(128)(4,1)} %bitcast.128), calls=%async_computation.7 | async-start | bytes 1048576
  431.4 15.0 %copy-start.5 = (bf16[1536,768]{1,0:T(8,128)(2,1)S(1)}, bf16[1536,768]{1,0:T(8,128)(2,1)}, u32[]{:S(2)}) copy-start(bf16[1536,768]{1,0:T(8,128)(2,1)} %get-tuple-element.32) | copy-start | bytes 7077892
  435.2 24.2 %collective-permute-start.12 = (bf16[4,24,3200]{2,1,0:T(8,128)(2,1)}, bf16[4,24,3200]{2,1,0:T(8,128)(2,1)S(1)}, u32[]{:S(2)}, u32[]{:S(2)}) collective-permute-start(bf16[4,24,3200]{2,1,0:T(8,128)(2,1)} %get-tuple-element.165), channel_id=1, source_target_pairs={{0,2},{2,0},{4,6},{6,4},{8,10},{10,8},{12,14},{14,12},{16,18},{18,... | collective-permute-start | bytes 1843208 | tf_op jit(solution)/shard_map/ppermute | solution.py:61
  444.6 29.1 %collective-permute-start.14 = (bf16[4,24,3200]{2,1,0:T(8,128)(2,1)}, bf16[4,24,3200]{2,1,0:T(8,128)(2,1)}, u32[]{:S(2)}, u32[]{:S(2)}) collective-permute-start(bf16[4,24,3200]{2,1,0:T(8,128)(2,1)} %get-tuple-element.166), channel_id=1, source_target_pairs={{0,6},{2,4},{4,2},{6,0},{8,14},{10,12},{12,10},{14,8},{16,22},{18,... | collective-permute-start | bytes 1843208 | tf_op jit(solution)/shard_map/ppermute | solution.py:61
  446.4 28.7 %collective-permute-start.13 = (bf16[4,24,3200]{2,1,0:T(8,128)(2,1)}, bf16[4,24,3200]{2,1,0:T(8,128)(2,1)}, u32[]{:S(2)}, u32[]{:S(2)}) collective-permute-start(bf16[4,24,3200]{2,1,0:T(8,128)(2,1)} %get-tuple-element.167), channel_id=1, source_target_pairs={{0,4},{2,6},{4,0},{6,2},{8,12},{10,14},{12,8},{14,10},{16,20},{18,... | collective-permute-start | bytes 1843208 | tf_op jit(solution)/shard_map/ppermute | solution.py:61
  476.7 8.4 %collective-permute-start.15 = (bf16[1,24,3200]{2,1,0:T(8,128)(2,1)S(1)}, bf16[1,24,3200]{2,1,0:T(8,128)(2,1)S(1)}, u32[]{:S(2)}, u32[]{:S(2)}) collective-permute-start(bf16[1,24,3200]{2,1,0:T(8,128)(2,1)S(1)} %get-tuple-element.168), channel_id=1, source_target_pairs={{0,8},{2,10},{4,12},{6,14},{8,0},{10,2},{12,4},{14,6},{16,24},{18,... | collective-permute-start | bytes 460808 | tf_op jit(solution)/shard_map/ppermute | solution.py:61
  478.2 8.7 %collective-permute-start.17 = (bf16[1,24,3200]{2,1,0:T(8,128)(2,1)S(1)}, bf16[1,24,3200]{2,1,0:T(8,128)(2,1)S(1)}, u32[]{:S(2)}, u32[]{:S(2)}) collective-permute-start(bf16[1,24,3200]{2,1,0:T(8,128)(2,1)S(1)} %get-tuple-element.169), channel_id=1, source_target_pairs={{0,24},{2,26},{4,28},{6,30},{8,16},{10,18},{12,20},{14,22},{16,8},... | collective-permute-start | bytes 460808 | tf_op jit(solution)/shard_map/ppermute | solution.py:61
  479.0 13.5 %collective-permute-start.16 = (bf16[1,24,3200]{2,1,0:T(8,128)(2,1)S(1)}, bf16[1,24,3200]{2,1,0:T(8,128)(2,1)S(1)}, u32[]{:S(2)}, u32[]{:S(2)}) collective-permute-start(bf16[1,24,3200]{2,1,0:T(8,128)(2,1)S(1)} %get-tuple-element.170), channel_id=1, source_target_pairs={{0,16},{2,18},{4,20},{6,22},{8,24},{10,26},{12,28},{14,30},{16,0},... | collective-permute-start | bytes 460808 | tf_op jit(solution)/shard_map/ppermute | solution.py:61
Sparse Core Ops, SparseCore 0:
  11.9 104.6 all-gather.1
  309.1 133.5 reduce-scatter.1
